TPU v7x, 512 devices: a whole 4x8x8 slice. The times are simulated.
512 devices in a mesh: patch: 4 (over x), shot: 128 (over z, y, core).
Axes of the slice: x: 4, y: 8, z: 8, core: 2. Of those that a mesh axis runs over, the one named last changes fastest.
Arguments:
- estimate: bfloat16 [256, 512, 1024], P('shot', 'patch'), may hold values from -6 to 6
- observed: bfloat16 [256, 512, 1024], P('shot', 'patch'), may hold values from -6 to 6
- random_source_delays: int32 [256], replicated, may hold values from 0 to 255
- thresholds: float32 [512], replicated, may hold values from 0.5 to 3
Outputs:
- updated: float32 [256, 512, 1024], P('shot', 'patch')
- misfit: float32 [256], P('shot')
All inputs are finite; a program needn't handle non-finite values.
Results may differ from a plain program's by a relative error of at most 0.0084.
Values may be sent and summed in bfloat16 or wider, within the bound.
A program may use at most 64 MiB of HBM per device.

v0:
```python
import jax
import jax.numpy as jnp
from jax import lax
from jax.sharding import PartitionSpec as P

NT = 1024
F = 512
SOURCE_SPACING = 512


correction_step_length = 0.5


def padded_2(shard, sides, width):
    for axis, dim in sides:
        peers, length = (lax.axis_size(axis), shard.shape[dim])
        up = [(i, (i + 1) % peers) for i in range(peers - 1)]
        down = [(j, i) for i, j in up]
        last = lax.slice_in_dim(shard, length - width, length, axis=dim)
        leading = lax.slice_in_dim(shard, 0, width, axis=dim)
        before = lax.ppermute(last, axis, up)
        after = lax.ppermute(leading, axis, down)
        shard = jnp.concatenate([before, shard, after], axis=dim)
    return shard


def delayed(traces, offset):
    length = traces.shape[-1]
    padded = jnp.pad(traces, ((0, 0), (length, length)))
    return lax.dynamic_slice_in_dim(padded, length - offset, length, 1)


def combined_data_panel(
    extended_receiver_signal, source_onset_moments_extended, initial_source_panel
):
    source_ordinal = extended_receiver_signal.shape[0] - 2
    record_window = lax.dynamic_slice_in_dim(
        source_onset_moments_extended, initial_source_panel + 2, source_ordinal + 2
    )
    subsequent_source_panel = record_window[2:] - record_window[1:-1]
    prior_source_panel = record_window[1:-1] - record_window[:-2]
    center = extended_receiver_signal[1:-1]
    later = jax.vmap(delayed)(extended_receiver_signal[2:], subsequent_source_panel)
    earlier = jax.vmap(delayed)(extended_receiver_signal[:-2], -prior_source_panel)
    return center + later + earlier


def time_tables():
    freq = jnp.arange(F, dtype=jnp.int32)
    sample = jnp.arange(NT, dtype=jnp.int32)
    phase = (freq[:, None] * sample[None, :] % NT).astype(jnp.float32)
    angle = 2.0 * jnp.pi * phase / NT
    root = jnp.sqrt(jnp.float32(NT))
    forward = jnp.stack([jnp.cos(angle) / root, -jnp.sin(angle) / root]).astype(jnp.bfloat16)
    weight = jnp.where(freq == 0, 1.0, 2.0).astype(jnp.float32)[:, None] / root
    inverse = jnp.stack([weight * jnp.cos(angle), -weight * jnp.sin(angle)]).astype(jnp.bfloat16)
    return (forward, inverse)


def shot_tables(source_panels):
    index = jnp.arange(source_panels, dtype=jnp.int32)
    phase = (index[:, None] * index[None, :] % source_panels).astype(jnp.float32)
    angle = 2.0 * jnp.pi * phase / source_panels
    root = jnp.sqrt(jnp.float32(source_panels))
    cosine = jnp.cos(angle) / root
    sine = jnp.sin(angle) / root
    across = jnp.stack([jnp.stack([cosine, sine]), jnp.stack([-sine, cosine])]).astype(jnp.bfloat16)
    back = jnp.stack([jnp.stack([cosine, -sine]), jnp.stack([sine, cosine])]).astype(jnp.bfloat16)
    return (across, back)


def shrink(wavenum, level):
    magnitude = jnp.sqrt(wavenum[0] * wavenum[0] + wavenum[1] * wavenum[1])
    factor = jnp.maximum(magnitude - level, 0.0) / jnp.maximum(magnitude, level)
    return (wavenum * factor[None]).astype(jnp.bfloat16)


def local(estimate, observed, random_source_delays, thresholds):
    shots_here = estimate.shape[0]
    total_sources = random_source_delays.shape[0]
    initial_source_panel = lax.axis_index("shot") * shots_here
    source_onset_moments = (
        jnp.arange(total_sources, dtype=jnp.int32) * SOURCE_SPACING + random_source_delays
    )
    source_onset_moments_extended = jnp.pad(source_onset_moments, (3, 3), mode="edge")
    present_gather = estimate.astype(jnp.float32)
    early_source_approximation = padded_2(estimate, (("shot", 0),), 1)
    resid = observed.astype(jnp.float32) - combined_data_panel(
        early_source_approximation.astype(jnp.float32),
        source_onset_moments_extended,
        initial_source_panel,
    )
    misfit_margin_samples = padded_2(resid, (("shot", 0),), 1)
    energy = jnp.sum(resid * resid, axis=(1, 2))
    misfit = lax.psum(energy, "patch") / (resid.shape[1] * lax.axis_size("patch") * NT)
    advanced_estimate = (
        present_gather
        + correction_step_length
        * combined_data_panel(
            misfit_margin_samples, source_onset_moments_extended, initial_source_panel
        )
    ).astype(jnp.bfloat16)
    forward, inverse = time_tables()
    spectra = jnp.einsum(
        "srt,pft->pfsr", advanced_estimate, forward, preferred_element_type=jnp.float32
    ).astype(jnp.bfloat16)
    share = F // lax.axis_size("shot")
    level = lax.dynamic_slice_in_dim(thresholds, lax.axis_index("shot") * share, share)
    across, back = shot_tables(total_sources)
    wavenum = jnp.einsum(
        "pqks,qfsr->pfkr",
        across,
        lax.all_to_all(spectra, "shot", split_axis=1, concat_axis=2, tiled=True),
        preferred_element_type=jnp.float32,
    )
    shrunk = shrink(wavenum, level[:, None, None])
    restored = jnp.einsum(
        "pqks,qfsr->pfkr", back, shrunk, preferred_element_type=jnp.float32
    ).astype(jnp.bfloat16)
    restored_here = lax.all_to_all(restored, "shot", split_axis=2, concat_axis=1, tiled=True)
    updated = jnp.einsum(
        "pft,pfsr->srt", inverse, restored_here, preferred_element_type=jnp.float32
    )
    return (updated, misfit)


def solution(mesh):
    in_specs = (P("shot", "patch", None), P("shot", "patch", None), P(), P())
    out_specs = (P("shot", "patch", None), P("shot"))
    return jax.shard_map(local, mesh=mesh, in_specs=in_specs, out_specs=out_specs, check_vma=False)
```

profile of v0, /device:TPU:1, one launch (start us, length us, event | category | flops | bytes accessed | tf_op | source)
XLA Modules:
  0.0 150.8 jit_solution(18273646294430069873)
XLA Ops:
  0.6 1.1 fusion.60
  1.7 4.6 %collective-permute-start = (bf16[1,128,1024]{2,1,0:T(8,128)(2,1)S(1)}, bf16[1,128,1024]{2,1,0:T(8,128)(2,1)S(1)}, u32[]{:S(2)}, u32[]{:S(2)}) collective-permute-start(bf16[1,128,1024]{2,1,0:T(8,128)(2,1)S(1)} %get-tuple-element.130), channel_id=1, source_target_pairs={{0,1},{1,2},{2,3},{3,4},{4,5},{5,6},{6,7},{7,8},{8,9},{9,10},{10,1... | collective-permute-start | bytes 786440 | tf_op jit(solution)/shard_map/ppermute | solution.py:21
  6.3 5.5 %collective-permute-start.1 = (bf16[1,128,1024]{2,1,0:T(8,128)(2,1)S(1)}, bf16[1,128,1024]{2,1,0:T(8,128)(2,1)S(1)}, u32[]{:S(2)}, u32[]{:S(2)}) collective-permute-start(bf16[1,128,1024]{2,1,0:T(8,128)(2,1)S(1)} %get-tuple-element.131), channel_id=1, source_target_pairs={{1,0},{2,1},{3,2},{4,3},{5,4},{6,5},{7,6},{8,7},{9,8},{10,9},{11,1... | collective-permute-start | bytes 786440 | tf_op jit(solution)/shard_map/ppermute | solution.py:22
  11.8 0.7 multiply_add_fusion
  12.5 0.7 fusion.61
  13.2 0.6 reshape.245
  13.8 0.7 reshape.246
  14.8 0.1 copy.22
  14.9 0.1 copy.21
  15.0 1.2 maximum_convert_fusion
  16.2 1.1 fusion.58
  17.3 2.0 %pad.16 = f32[2,128,3072]{2,1,0:T(8,128)} pad(f32[2,128,1024]{2,1,0:T(8,128)S(1)} %get-tuple-element.125, f32[]{:T(128)} %constant.70.clone.1), padding=0_0x0_0x1024_1024 | pad | bytes 4194308 | tf_op jit(solution)/shard_map/vmap(jit(_pad))/pad | solution.py:29
  19.3 0.1 broadcast.391.clone
  19.4 6.3 %while.5 = (s32[]{:T(128)}, f32[2,128,3072]{2,1,0:T(8,128)}, s32[2,3]{1,0:T(2,128)S(1)}, f32[2,128,1024]{2,1,0:T(8,128)S(1)}, s32[]{:T(128)}) while((s32[]{:T(128)}, f32[2,128,3072]{2,1,0:T(8,128)}, s32[2,3]{1,0:T(2,128)S(1)}, f32[2,128,1024]{2,1,0:T(8,128)S(1)}, s32[]{:T(128)}) %tuple.92), condition=%wide.while_cond.1, body=%wide.while_body.1.sunk | while | flops 2 | bytes 1048693 | solution.py:30
  19.5 0.6 fusion.68
  20.1 2.5 %dynamic-slice_dynamic-update-slice_fusion.9 = f32[2,128,1024]{2,1,0:T(8,128)S(1)} fusion(f32[2,128,1024]{2,1,0:T(8,128)S(1)} %get-tuple-element.274, s32[]{:T(128)} %get-tuple-element.271, f32[2,128,3072]{2,1,0:T(8,128)} %get-tuple-element.277, s32[]{:T(128)} %bitcast.89, s32[]{:T(128)} %bitcast.90), kind=kLoop, calls=%fused_computation.2.clone.1 | loop fusion | bytes 1048588 | tf_op jit(solution)/shard_map/vmap()/gather
  22.6 0.6 fusion.68
  23.2 2.5 %dynamic-slice_dynamic-update-slice_fusion.9 = f32[2,128,1024]{2,1,0:T(8,128)S(1)} fusion(f32[2,128,1024]{2,1,0:T(8,128)S(1)} %get-tuple-element.274, s32[]{:T(128)} %get-tuple-element.271, f32[2,128,3072]{2,1,0:T(8,128)} %get-tuple-element.277, s32[]{:T(128)} %bitcast.89, s32[]{:T(128)} %bitcast.90), kind=kLoop, calls=%fused_computation.2.clone.1 | loop fusion | bytes 1048588 | tf_op jit(solution)/shard_map/vmap()/gather
  25.7 3.2 %pad.15 = f32[2,128,3072]{2,1,0:T(8,128)} pad(f32[2,128,1024]{2,1,0:T(8,128)} %get-tuple-element.124, f32[]{:T(128)} %constant.70.clone.1), padding=0_0x0_0x1024_1024 | pad | bytes 4194308 | tf_op jit(solution)/shard_map/vmap(jit(_pad))/pad | solution.py:29
  29.0 1.1 broadcast.391.clone.1
  30.1 7.9 %while.4 = (s32[]{:T(128)}, f32[2,128,3072]{2,1,0:T(8,128)}, s32[2,3]{1,0:T(2,128)S(1)}, f32[2,128,1024]{2,1,0:T(8,128)}, s32[]{:T(128)}) while((s32[]{:T(128)}, f32[2,128,3072]{2,1,0:T(8,128)}, s32[2,3]{1,0:T(2,128)S(1)}, f32[2,128,1024]{2,1,0:T(8,128)}, s32[]{:T(128)}) %tuple.95), condition=%wide.while_cond, body=%wide.while_body.sunk | while | flops 2 | bytes 1050217 | solution.py:30
  30.1 0.6 fusion.67
  30.7 3.3 %dynamic-slice_dynamic-update-slice_fusion.8 = f32[2,128,1024]{2,1,0:T(8,128)} fusion(f32[2,128,1024]{2,1,0:T(8,128)} %get-tuple-element.289, s32[]{:T(128)} %get-tuple-element.286, f32[2,128,3072]{2,1,0:T(8,128)} %get-tuple-element.292, s32[]{:T(128)} %bitcast.87, s32[]{:T(128)} %bitcast.88), kind=kLoop, calls=%fused_computation.clone.1 | loop fusion | bytes 1050112 | tf_op jit(solution)/shard_map/vmap()/gather
  34.0 0.6 fusion.67
  34.6 3.3 %dynamic-slice_dynamic-update-slice_fusion.8 = f32[2,128,1024]{2,1,0:T(8,128)} fusion(f32[2,128,1024]{2,1,0:T(8,128)} %get-tuple-element.289, s32[]{:T(128)} %get-tuple-element.286, f32[2,128,3072]{2,1,0:T(8,128)} %get-tuple-element.292, s32[]{:T(128)} %bitcast.87, s32[]{:T(128)} %bitcast.88), kind=kLoop, calls=%fused_computation.clone.1 | loop fusion | bytes 1050112 | tf_op jit(solution)/shard_map/vmap()/gather
  37.9 1.7 %multiply_reduce_fusion = (f32[2]{0:T(128)S(1)}, f32[2,128,1024]{2,1,0:T(8,128)S(1)}) fusion(f32[2,128,1024]{2,1,0:T(8,128)S(1)} %get-tuple-element.17, f32[2,128,1024]{2,1,0:T(8,128)} %get-tuple-element.9, f32[4,128,1024]{2,1,0:T(8,128)S(1)} %maximum_convert_fusion, bf16[2,128,1024]{2,1,0:T(8,128)(2,1)} %param.5), kind=kLoop, calls=%fused_computation.44 | loop fusion | flops 1572862 | bytes 4718600 | tf_op jit(solution)/shard_map/reduce_sum | solution.py:94
  39.6 1.0 copy-done
  40.6 0.1 fusion.59
  40.7 1.9 %collective-permute-start.2 = (f32[1,128,1024]{2,1,0:T(8,128)S(1)}, f32[1,128,1024]{2,1,0:T(8,128)S(1)}, u32[]{:S(2)}, u32[]{:S(2)}) collective-permute-start(f32[1,128,1024]{2,1,0:T(8,128)S(1)} %get-tuple-element.128), channel_id=1, source_target_pairs={{1,0},{2,1},{3,2},{4,3},{5,4},{6,5},{7,6},{8,7},{9,8},{10,9},{11,1... | collective-permute-start | bytes 1572872 | tf_op jit(solution)/shard_map/ppermute | solution.py:22
  42.6 3.6 %collective-permute-start.3 = (f32[1,128,1024]{2,1,0:T(8,128)S(1)}, f32[1,128,1024]{2,1,0:T(8,128)}, u32[]{:S(2)}, u32[]{:S(2)}) collective-permute-start(f32[1,128,1024]{2,1,0:T(8,128)S(1)} %get-tuple-element.129), channel_id=1, source_target_pairs={{0,1},{1,2},{2,3},{3,4},{4,5},{5,6},{6,7},{7,8},{8,9},{9,10},{10,1... | collective-permute-start | bytes 1572872 | tf_op jit(solution)/shard_map/ppermute | solution.py:21
  46.3 9.3 %multiply_convert_fusion.2 = (bf16[1,512,1024]{2,1,0:T(8,128)(2,1)}, bf16[1,512,1024]{2,1,0:T(8,128)(2,1)}) fusion(), kind=kLoop, calls=%fused_computation.29 | loop fusion | flops 9961472 | bytes 2097152 | tf_op jit(solution)/shard_map/convert.19
  55.6 0.8 copy-done.2
  56.4 3.6 %select_maximum_fusion.1 = (f32[2,128,3072]{2,1,0:T(8,128)}, f32[2,128,3072]{2,1,0:T(8,128)S(1)}) fusion(f32[1,128,1024]{2,1,0:T(8,128)} %copy-done.2, f32[2,128,1024]{2,1,0:T(8,128)S(1)} %copy-done.1, f32[1,128,1024]{2,1,0:T(8,128)} %collective-permute-done.3), kind=kLoop, calls=%fused_computation.11 | loop fusion | flops 7077888 | bytes 8388608 | tf_op jit(solution)/shard_map/concatenate | solution.py:23
  60.1 1.1 broadcast.391.clone.3
  61.2 8.0 %while.6 = (s32[]{:T(128)}, f32[2,128,3072]{2,1,0:T(8,128)}, s32[2,3]{1,0:T(2,128)S(1)}, f32[2,128,1024]{2,1,0:T(8,128)}, s32[]{:T(128)}) while((s32[]{:T(128)}, f32[2,128,3072]{2,1,0:T(8,128)}, s32[2,3]{1,0:T(2,128)S(1)}, f32[2,128,1024]{2,1,0:T(8,128)}, s32[]{:T(128)}) %tuple.105), condition=%wide.while_cond.2, body=%wide.while_body.2.sunk | while | flops 2 | bytes 1050217 | solution.py:30
  61.2 0.7 fusion.69
  61.8 3.3 %dynamic-slice_dynamic-update-slice_fusion.10 = f32[2,128,1024]{2,1,0:T(8,128)} fusion(f32[2,128,1024]{2,1,0:T(8,128)} %get-tuple-element.319, s32[]{:T(128)} %get-tuple-element.316, f32[2,128,3072]{2,1,0:T(8,128)} %get-tuple-element.322, s32[]{:T(128)} %bitcast.91, s32[]{:T(128)} %bitcast.92), kind=kLoop, calls=%fused_computation.4.clone.1 | loop fusion | bytes 1050112 | tf_op jit(solution)/shard_map/vmap()/gather
  65.2 0.7 fusion.69
  65.8 3.3 %dynamic-slice_dynamic-update-slice_fusion.10 = f32[2,128,1024]{2,1,0:T(8,128)} fusion(f32[2,128,1024]{2,1,0:T(8,128)} %get-tuple-element.319, s32[]{:T(128)} %get-tuple-element.316, f32[2,128,3072]{2,1,0:T(8,128)} %get-tuple-element.322, s32[]{:T(128)} %bitcast.91, s32[]{:T(128)} %bitcast.92), kind=kLoop, calls=%fused_computation.4.clone.1 | loop fusion | bytes 1050112 | tf_op jit(solution)/shard_map/vmap()/gather
  69.2 1.1 broadcast.391.clone.2
  70.3 5.7 %while.7 = (s32[]{:T(128)}, f32[2,128,3072]{2,1,0:T(8,128)S(1)}, s32[2,3]{1,0:T(2,128)S(1)}, f32[2,128,1024]{2,1,0:T(8,128)}, s32[]{:T(128)}) while((s32[]{:T(128)}, f32[2,128,3072]{2,1,0:T(8,128)S(1)}, s32[2,3]{1,0:T(2,128)S(1)}, f32[2,128,1024]{2,1,0:T(8,128)}, s32[]{:T(128)}) %tuple.104), condition=%wide.while_cond.3, body=%wide.while_body.3.sunk | while | flops 2 | bytes 1050217 | solution.py:30
  70.3 0.6 fusion.70
  70.9 2.2 %dynamic-slice_dynamic-update-slice_fusion.11 = f32[2,128,1024]{2,1,0:T(8,128)} fusion(f32[2,128,1024]{2,1,0:T(8,128)} %get-tuple-element.304, s32[]{:T(128)} %get-tuple-element.301, f32[2,128,3072]{2,1,0:T(8,128)S(1)} %get-tuple-element.307, s32[]{:T(128)} %bitcast.93, s32[]{:T(128)} %bitcast.94), kind=kLoop, calls=%fused_computation.6.clone.1 | loop fusion | bytes 1050112 | tf_op jit(solution)/shard_map/vmap()/gather
  73.2 0.6 fusion.70
  73.8 2.2 %dynamic-slice_dynamic-update-slice_fusion.11 = f32[2,128,1024]{2,1,0:T(8,128)} fusion(f32[2,128,1024]{2,1,0:T(8,128)} %get-tuple-element.304, s32[]{:T(128)} %get-tuple-element.301, f32[2,128,3072]{2,1,0:T(8,128)S(1)} %get-tuple-element.307, s32[]{:T(128)} %bitcast.93, s32[]{:T(128)} %bitcast.94), kind=kLoop, calls=%fused_computation.6.clone.1 | loop fusion | bytes 1050112 | tf_op jit(solution)/shard_map/vmap()/gather
  76.0 3.4 %fusion.14 = bf16[2,512,2,128]{3,1,2,0:T(8,128)(2,1)S(1)} fusion(bf16[1,512,1024]{2,1,0:T(8,128)(2,1)} %get-tuple-element.146, bf16[1,512,1024]{2,1,0:T(8,128)(2,1)} %get-tuple-element.147, f32[2,128,1024]{2,1,0:T(8,128)} %get-tuple-element.33, f32[2,128,1024]{2,1,0:T(8,128)} %copy-done, f32[2,128,1024]{2,1,0:T(8,128)} %get-tuple-element.25, ...), kind=kOutput, calls=%fused_computation.37 | convolution fusion | flops 542900224 | bytes 6291456 | tf_op jit(solution)/shard_map/srt,pft->pfsr/dot_general | solution.py:104
  79.5 1.3 copy.25
  80.8 18.5 %all-to-all-start = ((bf16[2,512,2,128]{3,2,0,1:T(2,128)(2,1)}), bf16[2,512,2,128]{3,2,0,1:T(2,128)(2,1)S(1)}, u32[]{:S(2)}, u32[]{:S(2)}) async-start(bf16[2,512,2,128]{3,2,0,1:T(2,128)(2,1)} %copy.25), calls=%async_computation | async-start | bytes 1048576 | tf_op jit(solution)/shard_map/all_to_all | solution.py:113
  99.3 0.8 dynamic_slice.8
  100.1 1.0 fusion.44
  101.1 1.1 negate_convert_fusion
  102.3 17.6 %all-to-all-done = bf16[2,512,2,128]{3,2,0,1:T(2,128)(2,1)S(1)} async-done(((bf16[2,512,2,128]{3,2,0,1:T(2,128)(2,1)}), bf16[2,512,2,128]{3,2,0,1:T(2,128)(2,1)S(1)}, u32[]{:S(2)}, u32[]{:S(2)}) %all-to-all-start) | async-done | bytes 524320 | tf_op jit(solution)/shard_map/all_to_all | solution.py:113
  119.9 0.4 copy.26
  120.2 0.5 convolution_bitcast_fusion.1
  120.7 0.3 divide_bitcast_fusion
  121.0 0.5 fusion.16
  121.5 1.2 copy.28
  122.7 5.5 %all-to-all-start.1 = ((bf16[2,4,256,128]{3,0,1,2:T(2,128)(2,1)}), bf16[2,4,256,128]{3,0,1,2:T(2,128)(2,1)S(1)}, u32[]{:S(2)}, u32[]{:S(2)}) async-start(bf16[2,4,256,128]{3,0,1,2:T(2,128)(2,1)} %copy.28), calls=%async_computation.1 | async-start | bytes 1048576 | tf_op jit(solution)/shard_map/all_to_all | solution.py:120
  128.2 8.7 %multiply_convert_fusion = (bf16[1,512,1024]{2,1,0:T(8,128)(2,1)S(1)}, bf16[1,512,1024]{2,1,0:T(8,128)(2,1)S(1)}) fusion(f32[512]{0:T(512)S(1)} %fusion.45, f32[512]{0:T(512)S(1)} %select_multiply_fusion), kind=kLoop, calls=%fused_computation.27 | loop fusion | flops 9437184 | bytes 2101248 | tf_op jit(solution)/shard_map/convert.1
  136.9 9.1 %psum.7 = f32[2]{0:T(128)S(1)} all-reduce(f32[2]{0:T(128)S(1)} %get-tuple-element.114), channel_id=1, replica_groups=mesh['patch'=4,'shot'=128] {'patch'}, use_global_device_ids=true, to_apply=%region_1.2 | all-reduce | flops 2 | bytes 16 | tf_op jit(solution)/shard_map/psum | solution.py:95
  145.9 0.5 broadcast_multiply_fusion
  146.5 2.2 %all-to-all-done.1 = bf16[2,4,256,128]{3,0,1,2:T(2,128)(2,1)S(1)} async-done(((bf16[2,4,256,128]{3,0,1,2:T(2,128)(2,1)}), bf16[2,4,256,128]{3,0,1,2:T(2,128)(2,1)S(1)}, u32[]{:S(2)}, u32[]{:S(2)}) %all-to-all-start.1) | async-done | bytes 524320 | tf_op jit(solution)/shard_map/all_to_all | solution.py:120
  148.7 0.4 copy.30
  149.1 1.7 %fusion.13 = f32[2,128,1024]{2,1,0:T(8,128)} fusion(bf16[2,512,2,128]{3,1,2,0:T(8,128)(2,1)S(1)} %bitcast.97, bf16[1,512,1024]{2,1,0:T(8,128)(2,1)S(1)} %get-tuple-element.148, bf16[1,512,1024]{2,1,0:T(8,128)(2,1)S(1)} %get-tuple-element.149), kind=kOutput, calls=%fused_computation.34 | convolution fusion | flops 537919488 | bytes 3670016 | tf_op jit(solution)/shard_map/pft,pfsr->srt/dot_general | solution.py:121
  (25 shorter events, 0.5 us)
Async XLA Ops:
  1.7 13.3 %collective-permute-start = (bf16[1,128,1024]{2,1,0:T(8,128)(2,1)S(1)}, bf16[1,128,1024]{2,1,0:T(8,128)(2,1)S(1)}, u32[]{:S(2)}, u32[]{:S(2)}) collective-permute-start(bf16[1,128,1024]{2,1,0:T(8,128)(2,1)S(1)} %get-tuple-element.130), channel_id=1, source_target_pairs={{0,1},{1,2},{2,3},{3,4},{4,5},{5,6},{6,7},{7,8},{8,9},{9,10},{10,1... | collective-permute-start | bytes 786440 | tf_op jit(solution)/shard_map/ppermute | solution.py:21
  6.3 8.7 %collective-permute-start.1 = (bf16[1,128,1024]{2,1,0:T(8,128)(2,1)S(1)}, bf16[1,128,1024]{2,1,0:T(8,128)(2,1)S(1)}, u32[]{:S(2)}, u32[]{:S(2)}) collective-permute-start(bf16[1,128,1024]{2,1,0:T(8,128)(2,1)S(1)} %get-tuple-element.131), channel_id=1, source_target_pairs={{1,0},{2,1},{3,2},{4,3},{5,4},{6,5},{7,6},{8,7},{9,8},{10,9},{11,1... | collective-permute-start | bytes 786440 | tf_op jit(solution)/shard_map/ppermute | solution.py:22
  39.6 1.0 copy-start
  40.7 14.9 %collective-permute-start.2 = (f32[1,128,1024]{2,1,0:T(8,128)S(1)}, f32[1,128,1024]{2,1,0:T(8,128)S(1)}, u32[]{:S(2)}, u32[]{:S(2)}) collective-permute-start(f32[1,128,1024]{2,1,0:T(8,128)S(1)} %get-tuple-element.128), channel_id=1, source_target_pairs={{1,0},{2,1},{3,2},{4,3},{5,4},{6,5},{7,6},{8,7},{9,8},{10,9},{11,1... | collective-permute-start | bytes 1572872 | tf_op jit(solution)/shard_map/ppermute | solution.py:22
  42.6 13.8 %collective-permute-start.3 = (f32[1,128,1024]{2,1,0:T(8,128)S(1)}, f32[1,128,1024]{2,1,0:T(8,128)}, u32[]{:S(2)}, u32[]{:S(2)}) collective-permute-start(f32[1,128,1024]{2,1,0:T(8,128)S(1)} %get-tuple-element.129), channel_id=1, source_target_pairs={{0,1},{1,2},{2,3},{3,4},{4,5},{5,6},{6,7},{7,8},{8,9},{9,10},{10,1... | collective-permute-start | bytes 1572872 | tf_op jit(solution)/shard_map/ppermute | solution.py:21
  46.3 10.1 %copy-start.1 = (f32[2,128,1024]{2,1,0:T(8,128)S(1)}, f32[2,128,1024]{2,1,0:T(8,128)}, u32[]{:S(2)}) copy-start(f32[2,128,1024]{2,1,0:T(8,128)} %copy-done) | copy-start | bytes 3145732
  55.6 0.8 copy-start.2
  80.8 39.1 %all-to-all-start = ((bf16[2,512,2,128]{3,2,0,1:T(2,128)(2,1)}), bf16[2,512,2,128]{3,2,0,1:T(2,128)(2,1)S(1)}, u32[]{:S(2)}, u32[]{:S(2)}) async-start(bf16[2,512,2,128]{3,2,0,1:T(2,128)(2,1)} %copy.25), calls=%async_computation | async-start | bytes 1048576 | tf_op jit(solution)/shard_map/all_to_all | solution.py:113
  122.7 26.0 %all-to-all-start.1 = ((bf16[2,4,256,128]{3,0,1,2:T(2,128)(2,1)}), bf16[2,4,256,128]{3,0,1,2:T(2,128)(2,1)S(1)}, u32[]{:S(2)}, u32[]{:S(2)}) async-start(bf16[2,4,256,128]{3,0,1,2:T(2,128)(2,1)} %copy.28), calls=%async_computation.1 | async-start | bytes 1048576 | tf_op jit(solution)/shard_map/all_to_all | solution.py:120
where the time goes:
time: 152 us; the launch traced here: 151 us
  local copies, waits for them, and re-layouts  47 us (31%)
  starting transfers between devices  39.6 us (26%)
  other arithmetic  28.3 us (19%)
  waiting for transfers between devices  19.8 us (13%)
  blocking collectives  9.07 us (6%)
  matrix products  6.08 us (4%)
    gather x24, local copies, waits for them, and re-layouts  27.8 us
    another operation x4, other arithmetic  20.1 us
    all_to_all x1, starting transfers between devices, local(): lax.all_to_all(spectra, 'shot', split_axis=1, concat_axis=2, tiled=True)  18.5 us
    all_to_all x1, waiting for transfers between devices, local(): lax.all_to_all(spectra, 'shot', split_axis=1, concat_axis=2, tiled=True)  17.6 us
    psum x1, blocking collectives, local(): lax.psum(energy, 'patch') / (resid.shape[1] * lax.axis_size('patch') * NT)  9.07 us
    ppermute x2, starting transfers between devices, padded_2(): before = lax.ppermute(last, axis, up)  8.24 us
    ppermute x2, starting transfers between devices, padded_2(): after = lax.ppermute(leading, axis, down)  7.42 us
    all_to_all x1, starting transfers between devices, local(): lax.all_to_all(restored, 'shot', split_axis=2, concat_axis=1, tiled=True)  5.49 us
  transfers between devices with their start and end apart: 6, of which 2 were waited for; matrix products, arithmetic and copies ran while one was open for 16% of the time, Pallas kernels for 0%

commit v1 on v0

v1 whole, which is shorter than its diff:
```python
import functools
import math

import jax
import jax.numpy as jnp
import ml_dtypes
import numpy as np
from jax import lax
from jax.experimental import pallas as pl
from jax.experimental.pallas import tpu as pltpu
from jax.sharding import PartitionSpec as P

SOURCE_SPACING = 512
LONGEST = 768
ROWS = 16
MESH = pl.DeviceIdType.MESH


def time_table(frequencies, samples):
    phase = np.arange(frequencies)[:, None] * np.arange(samples)[None, :] % samples
    angle = 2.0 * math.pi * phase / samples
    table = np.stack([np.cos(angle), -np.sin(angle)], axis=1) / math.sqrt(samples)
    return table.reshape(2 * frequencies, samples).astype(np.float32).astype(ml_dtypes.bfloat16)


def shot_table(shots, here):
    index = np.arange(shots).reshape(shots // here, here).T.reshape(-1)
    angle = 2.0 * math.pi * (index[:, None] * index[None, :] % shots) / shots
    table = np.concatenate([np.cos(angle), np.sin(angle)]) / math.sqrt(shots)
    return table.astype(np.float32).astype(ml_dtypes.bfloat16)


def shift_left(x, lane, offset):
    length = x.shape[1]
    return jnp.where(lane < length - offset, pltpu.roll(x, length - offset, 1), 0.0)


def shift_right(x, lane, offset):
    return jnp.where(lane >= offset, pltpu.roll(x, offset, 1), 0.0)


def kernel(
    dims,
    est_hbm, obs_hbm, delay_hbm, level_hbm, table_hbm, cn_hbm,
    out_hbm, misfit_ref,
    est, obs, delay, level, table, cn,
    halo_out, halo_in, partial, stepped, energy, energies,
    send1, recv1, wide1, wide2, send2, recv2, out,
    load_sem, store_sem, halo_send, halo_recv, plane_sem,
    send1_sem, recv1_sem, send2_sem, recv2_sem, energy_send, energy_recv,
):
    patches, n, rings, ring = dims
    shots, receivers, length = est.shape
    bands = wide1.shape[0] // n // 4
    me, x = lax.axis_index("shot"), lax.axis_index("patch")
    z, place = me // ring, me % ring
    right, left = (me + 1) % n, (me + n - 1) % n
    last = n * shots - 1

    loads = [
        pltpu.make_async_copy(src, dst, load_sem.at[i])
        for i, (src, dst) in enumerate(
            [(delay_hbm, delay), (est_hbm, est), (obs_hbm, obs), (level_hbm, level), (table_hbm, table), (cn_hbm, cn)]
        )
    ]
    for load in loads:
        load.start()

    barrier = pltpu.get_barrier_semaphore()

    def greet_ring(i, carry):
        pl.semaphore_signal(barrier, 1, device_id={"shot": z * ring + (place + i) % ring}, device_id_type=MESH)
        return carry

    def greet_planes(i, carry):
        pl.semaphore_signal(barrier, 1, device_id={"shot": (z + i) % rings * ring + place}, device_id_type=MESH)
        return carry

    def greet_patches(i, carry):
        pl.semaphore_signal(barrier, 1, device_id={"patch": (x + i) % patches}, device_id_type=MESH)
        return carry

    pl.semaphore_signal(barrier, 1, device_id={"shot": right}, device_id_type=MESH)
    pl.semaphore_signal(barrier, 1, device_id={"shot": left}, device_id_type=MESH)
    lax.fori_loop(1, ring, greet_ring, 0)
    lax.fori_loop(1, rings, greet_planes, 0)
    lax.fori_loop(1, patches, greet_patches, 0)

    loads[0].wait()
    first = me * shots
    d_before = delay[jnp.maximum(first - 1, 0)]
    d_0 = delay[first]
    d_1 = delay[first + 1]
    d_after = delay[jnp.minimum(first + 2, last)]
    a_before = SOURCE_SPACING + d_0 - d_before
    a_here = SOURCE_SPACING + d_1 - d_0
    a_after = SOURCE_SPACING + d_after - d_1
    lane = lax.broadcasted_iota(jnp.int32, (ROWS, length), 1)
    loads[1].wait()
    loads[2].wait()

    def before_halo(i, carry):
        rows = pl.ds(i * ROWS, ROWS)
        e0 = est[0, rows, :].astype(jnp.float32)
        e1 = est[1, rows, :].astype(jnp.float32)
        p0 = obs[0, rows, :].astype(jnp.float32) - e0 - shift_right(e1, lane, a_here)
        p1 = obs[1, rows, :].astype(jnp.float32) - e1 - shift_left(e0, lane, a_here)
        partial[0, rows, :] = p0
        partial[1, rows, :] = p1
        halo_out[0, 0, rows, :] = shift_left(e1, lane, a_after)[:, :LONGEST].astype(jnp.bfloat16)
        halo_out[0, 1, rows, :] = shift_left(p1, lane, a_after)[:, :LONGEST].astype(jnp.bfloat16)
        halo_out[1, 0, rows, :] = shift_right(e0, lane, a_before)[:, length - LONGEST :].astype(jnp.bfloat16)
        halo_out[1, 1, rows, :] = shift_right(p0, lane, a_before)[:, length - LONGEST :].astype(jnp.bfloat16)
        return carry

    lax.fori_loop(0, receivers // ROWS, before_halo, 0)

    pl.semaphore_wait(barrier, ring - 1 + rings - 1 + patches - 1 + 2)

    halos = [
        pltpu.make_async_remote_copy(
            halo_out.at[side], halo_in.at[side], halo_send.at[side], halo_recv.at[side],
            device_id={"shot": peer}, device_id_type=MESH,
        )
        for side, peer in enumerate([right, left])
    ]
    for halo in halos:
        halo.start()

    def plane_ready(i, carry):
        pl.semaphore_signal(plane_sem, 1, device_id={"shot": (z + i) % rings * ring + place}, device_id_type=MESH)
        return carry

    lax.fori_loop(1, rings, plane_ready, 0)
    for load in loads[3:]:
        load.wait()
    for halo in halos:
        halo.wait_recv()

    def after_halo(i, carry):
        rows = pl.ds(i * ROWS, ROWS)
        e0 = est[0, rows, :].astype(jnp.float32)
        e1 = est[1, rows, :].astype(jnp.float32)
        blank = jnp.zeros((ROWS, length - LONGEST), jnp.float32)
        has_left = me > 0
        has_right = me < n - 1

        def from_left(kind):
            got = halo_in[0, kind, rows, :].astype(jnp.float32)
            return jnp.concatenate([jnp.where(has_left, got, 0.0), blank], axis=1)

        def from_right(kind):
            got = halo_in[1, kind, rows, :].astype(jnp.float32)
            return jnp.concatenate([blank, jnp.where(has_right, got, 0.0)], axis=1)

        r0 = partial[0, rows, :] - from_left(0)
        r1 = partial[1, rows, :] - from_right(0)
        own0 = jnp.where(lane < jnp.where(has_left, length - a_before, 0), e0, 0.0)
        own1 = jnp.where(lane >= jnp.where(has_right, a_after, length), e1, 0.0)
        s0 = e0 + 0.5 * (r0 + shift_right(r1, lane, a_here) + (from_left(1) - own0))
        s1 = e1 + 0.5 * (r1 + shift_left(r0, lane, a_here) + (from_right(1) - own1))
        stepped[rows, :] = s0.astype(jnp.bfloat16)
        stepped[pl.ds(receivers + i * ROWS, ROWS), :] = s1.astype(jnp.bfloat16)

        def squares(r):
            total = jnp.zeros((8, 128), jnp.float32)
            for a in range(0, ROWS, 8):
                for b in range(0, length, 128):
                    piece = r[a : a + 8, b : b + 128]
                    total = total + piece * piece
            return total

        return carry[0] + squares(r0), carry[1] + squares(r1)

    zero = jnp.zeros((8, 128), jnp.float32)
    e_0, e_1 = lax.fori_loop(0, receivers // ROWS, after_halo, (zero, zero))
    energy[0] = e_0
    energy[1] = e_1

    pl.semaphore_wait(plane_sem, rings - 1)

    def planes(offsets):
        field = stepped[...]
        for dz in offsets:
            zz = (z + dz) % rings
            rows = table[pl.ds(pl.multiple_of(zz * (ring * 8), ring * 8), ring * 8), :]
            got = lax.dot_general(rows, field, (((1,), (1,)), ((), ())), preferred_element_type=jnp.float32)
            tiles = [got[:, s * receivers : (s + 1) * receivers].reshape(ring, 8, receivers) for s in range(shots)]
            send1[pl.ds(zz * ring, ring)] = jnp.concatenate(tiles, axis=1).astype(jnp.bfloat16)

    def send_planes(offsets, src, dst, ssem, rsem):
        def one(i, carry):
            for dz in offsets:
                peer = (z + dz) % rings * ring + (place + i) % ring
                pltpu.make_async_remote_copy(
                    src(peer), dst(me), ssem, rsem, device_id={"shot": peer}, device_id_type=MESH
                ).start()
            return carry

        if 0 in offsets:
            far = tuple(dz for dz in offsets if dz)
            for dz in far:
                peer = (z + dz) % rings * ring + place
                pltpu.make_async_remote_copy(
                    src(peer), dst(me), ssem, rsem, device_id={"shot": peer}, device_id_type=MESH
                ).start()
            pltpu.make_async_copy(src(me), dst(me), rsem).start()
            lax.fori_loop(1, ring, one, 0)
        else:
            lax.fori_loop(0, ring, one, 0)

    half = rings // 2
    groups = [(half, 0)] + [(dz, rings - dz) for dz in range(half - 1, 0, -1)]
    for offsets in groups:
        planes(offsets)
        send_planes(offsets, lambda d: send1.at[d], lambda d: recv1.at[d], send1_sem, recv1_sem)

    for i in range(1, patches):
        pltpu.make_async_remote_copy(
            energy, energies.at[x], energy_send.at[i], energy_recv,
            device_id={"patch": (x + i) % patches}, device_id_type=MESH,
        ).start()
    pltpu.make_async_copy(energy, energies.at[x], energy_recv).start()

    pltpu.make_async_copy(recv1, recv1, recv1_sem).wait()

    wide1[...] = recv1[...].astype(jnp.float32).reshape(wide1.shape)
    wave = cn[...]
    k = n * shots
    for band in range(bands):
        columns = []
        for q in range(2):
            parts = [wide1[pl.ds(s * 8 + band * 2 + q, n, stride=16), :] for s in range(shots)]
            columns.append(jnp.concatenate(parts, axis=0))
        field = jnp.concatenate(columns, axis=1).astype(jnp.bfloat16)
        got = jnp.dot(wave, field, preferred_element_type=jnp.float32)
        real = got[:k, :receivers] + got[k:, receivers:]
        imag = got[:k, receivers:] - got[k:, :receivers]
        f = me * bands + band
        limit = level[f]
        weight = jnp.where(f == 0, 1.0, 2.0)
        magnitude = jnp.sqrt(real * real + imag * imag)
        factor = jnp.maximum(magnitude - limit, 0.0) / jnp.maximum(magnitude, limit) * weight
        shrunk = jnp.concatenate([real * factor, imag * factor], axis=1).astype(jnp.bfloat16)
        got = jnp.dot(wave, shrunk, preferred_element_type=jnp.float32)
        real = got[:k, :receivers] - got[k:, receivers:]
        imag = got[:k, receivers:] + got[k:, :receivers]
        for s in range(shots):
            wide2[pl.ds(s * 8 + band * 2, n, stride=16), :] = real[s * n : (s + 1) * n]
            wide2[pl.ds(s * 8 + band * 2 + 1, n, stride=16), :] = imag[s * n : (s + 1) * n]
    tiles = wide2[...].reshape(n, 16, receivers)
    for s in range(shots):
        send2[s] = tiles[:, s * 8 : (s + 1) * 8, :].astype(jnp.bfloat16)
    for offsets in groups:
        send_planes(offsets, lambda d: send2.at[:, d], lambda d: recv2.at[:, d], send2_sem, recv2_sem)

    pltpu.make_async_copy(energies, energies, energy_recv).wait()
    total = energies[0]
    for i in range(1, patches):
        total = total + energies[i]
    for s in range(shots):
        misfit_ref[s] = jnp.sum(total[s]) / (patches * receivers * length)

    pltpu.make_async_copy(recv2, recv2, recv2_sem).wait()

    stores = []
    for s in range(shots):
        field = recv2[s].astype(jnp.float32).reshape(n * 8, receivers).astype(jnp.bfloat16)
        out[s] = lax.dot_general(field, table[...], (((0,), (0,)), ((), ())), preferred_element_type=jnp.float32)
        stores.append(pltpu.make_async_copy(out.at[s], out_hbm.at[s], store_sem.at[s]))
        stores[-1].start()

    for halo in halos:
        halo.wait_send()
    for i in range(1, patches):
        pltpu.make_async_remote_copy(
            energy, energies.at[x], energy_send.at[i], energy_recv,
            device_id={"patch": (x + i) % patches}, device_id_type=MESH,
        ).wait_send()
    rest = pl.ds(0, n - 1)
    pltpu.make_async_copy(send1.at[rest], send1.at[rest], send1_sem).wait()
    pltpu.make_async_copy(send2.at[:, rest], send2.at[:, rest], send2_sem).wait()
    for store in stores:
        store.wait()


def local(dims, estimate, observed, delays, thresholds):
    shots, receivers, length = estimate.shape
    n = dims[1]
    frequencies = thresholds.shape[0]
    bf16, f32 = jnp.bfloat16, jnp.float32
    table = jnp.asarray(time_table(frequencies, length))
    cn = jnp.asarray(shot_table(n * shots, shots))
    bands = frequencies // n
    sem = pltpu.SemaphoreType.DMA
    return pl.pallas_call(
        functools.partial(kernel, dims),
        out_shape=(
            jax.ShapeDtypeStruct((shots, receivers, length), f32),
            jax.ShapeDtypeStruct((shots,), f32),
        ),
        in_specs=[pl.BlockSpec(memory_space=pl.ANY)] * 6,
        out_specs=(pl.BlockSpec(memory_space=pl.ANY), pl.BlockSpec(memory_space=pltpu.SMEM)),
        scratch_shapes=[
            pltpu.VMEM(estimate.shape, bf16),
            pltpu.VMEM(estimate.shape, bf16),
            pltpu.SMEM(delays.shape, jnp.int32),
            pltpu.SMEM(thresholds.shape, f32),
            pltpu.VMEM(table.shape, bf16),
            pltpu.VMEM(cn.shape, bf16),
            pltpu.VMEM((2, 2, receivers, LONGEST), bf16),
            pltpu.VMEM((2, 2, receivers, LONGEST), bf16),
            pltpu.VMEM(estimate.shape, f32),
            pltpu.VMEM((shots * receivers, length), bf16),
            pltpu.VMEM((shots, 8, 128), f32),
            pltpu.VMEM((dims[0], shots, 8, 128), f32),
            pltpu.VMEM((n, 16, receivers), bf16),
            pltpu.VMEM((n, 16, receivers), bf16),
            pltpu.VMEM((n * 4 * bands, receivers), f32),
            pltpu.VMEM((n * 4 * bands, receivers), f32),
            pltpu.VMEM((shots, n, 8, receivers), bf16),
            pltpu.VMEM((shots, n, 8, receivers), bf16),
            pltpu.VMEM(estimate.shape, f32),
            sem((6,)),
            sem((shots,)),
            sem((2,)),
            sem((2,)),
            pltpu.SemaphoreType.REGULAR,
            sem,
            sem,
            sem,
            sem,
            sem((dims[0],)),
            sem,
        ],
        compiler_params=pltpu.CompilerParams(
            collective_id=0, has_side_effects=True, vmem_limit_bytes=48 * 2**20
        ),
    )(estimate, observed, delays, thresholds, table, cn)


def solution(mesh):
    patches, n = mesh.shape["patch"], mesh.shape["shot"]
    rings = 8
    dims = (patches, n, rings, n // rings)
    in_specs = (P("shot", "patch", None), P("shot", "patch", None), P(), P())
    out_specs = (P("shot", "patch", None), P("shot"))
    return jax.shard_map(
        functools.partial(local, dims), mesh=mesh, in_specs=in_specs, out_specs=out_specs, check_vma=False
    )
```

time: 152 us -> 64.3 us (0.42)
  Pallas kernels: 0 us -> 55.9 us
  starting transfers between devices: 39.6 us -> 0 us
  local copies, waits for them, and re-layouts: 47 us -> 7.46 us
  other arithmetic: 28.3 us -> 0 us
  waiting for transfers between devices: 19.8 us -> 0 us
  blocking collectives: 9.07 us -> 0 us
  matrix products: 6.08 us -> 0 us
    pallas_call x0 -> x1, Pallas kernels: none -> 55.9 us  [local(): pl.pallas_call(functools.partial(kernel, dims), out_shape=(jax.ShapeDtype...]
    gather x24 -> x0, local copies, waits for them, and re-layouts: 27.8 us -> none
    all_to_all x2 -> x0, starting transfers between devices: 24 us -> none  [the longest x1 18.5 us: local(): lax.all_to_all(spectra, 'shot', split_axis=1, concat_axis=2, tiled=True)]
    another operation x5 -> x0, other arithmetic: 20.2 us -> none
    all_to_all x2 -> x0, waiting for transfers between devices: 19.8 us -> none  [the longest x1 17.6 us: local(): lax.all_to_all(spectra, 'shot', split_axis=1, concat_axis=2, tiled=True)]
    ppermute x4 -> x0, starting transfers between devices: 15.7 us -> none  [the longest x2 8.24 us: padded_2(): before = lax.ppermute(last, axis, up)]
    psum x1 -> x0, blocking collectives: 9.07 us -> none  [local(): lax.psum(energy, 'patch') / (resid.shape[1] * lax.axis_size('patch') * NT)]
    dot_general x4 -> x0, matrix products: 6.08 us -> none  [the longest x1 3.42 us: local(): jnp.einsum('srt,pft->pfsr', advanced_estimate, forward, preferred_element...]
  transfers between devices with their start and end apart: 6 -> 0, of which waited for: 2 -> 0; matrix products, arithmetic and copies ran while one was open for 16% -> 0% of each run, Pallas kernels for 0% -> 0%
where the time goes in v1:
time: 64.3 us; the launch traced here: 64 us
  Pallas kernels  55.9 us (87%)
  local copies, waits for them, and re-layouts  7.46 us (12%)
  between operations  0.65 us (1%)
    pallas_call x1, Pallas kernels, local(): pl.pallas_call(functools.partial(kernel, dims), out_shape=(jax.ShapeDtype...  55.9 us
    unnamed x14, local copies, waits for them, and re-layouts  7.46 us

profile of v1, /device:TPU:1, one launch (start us, length us, event | category | flops | bytes accessed | tf_op | source)
XLA Modules:
  0.0 64.0 jit_solution(17761194044545119901)
XLA Ops:
  0.6 0.0 copy-start
  0.6 1.6 %copy-done = bf16[1024,1024]{1,0:T(8,128)(2,1)S(1)} copy-done((bf16[1024,1024]{1,0:T(8,128)(2,1)S(1)}, bf16[1024,1024]{1,0:T(8,128)(2,1)}, u32[]{:S(2)}) %copy-start) | copy-done | bytes 2097176
  2.2 0.0 copy-start.1
  2.2 1.0 %copy-done.1 = bf16[2,128,1024]{2,1,0:T(8,128)(2,1)S(1)} copy-done((bf16[2,128,1024]{2,1,0:T(8,128)(2,1)S(1)}, bf16[2,128,1024]{2,1,0:T(8,128)(2,1)}, u32[]{:S(2)}) %copy-start.1) | copy-done | bytes 524312
  3.3 0.0 copy-start.2
  3.3 1.0 %copy-done.2 = bf16[2,128,1024]{2,1,0:T(8,128)(2,1)S(1)} copy-done((bf16[2,128,1024]{2,1,0:T(8,128)(2,1)S(1)}, bf16[2,128,1024]{2,1,0:T(8,128)(2,1)}, u32[]{:S(2)}) %copy-start.2) | copy-done | bytes 524312
  4.3 0.0 copy-start.3
  4.3 0.9 %copy-done.3 = bf16[512,256]{1,0:T(8,128)(2,1)S(1)} copy-done((bf16[512,256]{1,0:T(8,128)(2,1)S(1)}, bf16[512,256]{1,0:T(8,128)(2,1)}, u32[]{:S(2)}) %copy-start.3) | copy-done | bytes 262168
  5.3 0.0 copy-start.4
  5.3 0.7 %copy-done.4 = f32[512]{0:T(512)S(1)} copy-done((f32[512]{0:T(512)S(1)}, f32[512]{0:T(512)}, u32[]{:S(2)}) %copy-start.4) | copy-done | bytes 2072
  5.9 0.0 copy-start.5
  5.9 0.7 %copy-done.5 = s32[256]{0:T(256)S(1)} copy-done((s32[256]{0:T(256)S(1)}, s32[256]{0:T(256)}, u32[]{:S(2)}) %copy-start.5) | copy-done | bytes 1048
  6.6 55.9 %shard_map.77 = (f32[2,128,1024]{2,1,0:T(8,128)S(1)}, f32[2]{0:T(128)S(1)}) custom-call(bf16[2,128,1024]{2,1,0:T(8,128)(2,1)S(1)} %copy-done.1, bf16[2,128,1024]{2,1,0:T(8,128)(2,1)S(1)} %copy-done.2, s32[256]{0:T(256)S(1)} %copy-done.5, f32[512]{0:T(512)S(1)} %copy-done.4, bf16[1024,1024]{1,0:T(8,128)(2,1)S(1)} %copy-done, bf16[512,256]{1,0:T(8,128)(2,1)S(1)} %copy-done.3), custom_call_target="tpu_custom_call" | custom-call | tf_op jit(solution)/shard_map/pallas_call | solution.py:296
  62.5 1.0 %copy.10 = f32[2,128,1024]{2,1,0:T(8,128)} copy(f32[2,128,1024]{2,1,0:T(8,128)S(1)} %get-tuple-element.4) | data formatting | bytes 2097152
  63.5 0.5 copy.11
Async XLA Ops:
  0.6 1.6 %copy-start = (bf16[1024,1024]{1,0:T(8,128)(2,1)S(1)}, bf16[1024,1024]{1,0:T(8,128)(2,1)}, u32[]{:S(2)}) copy-start(bf16[1024,1024]{1,0:T(8,128)(2,1)} %constant.4.clone.table_hbm) | copy-start | bytes 6291460
  2.2 1.0 %copy-start.1 = (bf16[2,128,1024]{2,1,0:T(8,128)(2,1)S(1)}, bf16[2,128,1024]{2,1,0:T(8,128)(2,1)}, u32[]{:S(2)}) copy-start(bf16[2,128,1024]{2,1,0:T(8,128)(2,1)} %est_hbm.1) | copy-start | bytes 1572868
  3.3 1.0 %copy-start.2 = (bf16[2,128,1024]{2,1,0:T(8,128)(2,1)S(1)}, bf16[2,128,1024]{2,1,0:T(8,128)(2,1)}, u32[]{:S(2)}) copy-start(bf16[2,128,1024]{2,1,0:T(8,128)(2,1)} %obs_hbm.1) | copy-start | bytes 1572868
  4.3 0.9 %copy-start.3 = (bf16[512,256]{1,0:T(8,128)(2,1)S(1)}, bf16[512,256]{1,0:T(8,128)(2,1)}, u32[]{:S(2)}) copy-start(bf16[512,256]{1,0:T(8,128)(2,1)} %constant.5.clone.cn_hbm) | copy-start | bytes 786436
  5.3 0.7 %copy-start.4 = (f32[512]{0:T(512)S(1)}, f32[512]{0:T(512)}, u32[]{:S(2)}) copy-start(f32[512]{0:T(512)} %level_hbm.1) | copy-start | bytes 6148
  5.9 0.7 %copy-start.5 = (s32[256]{0:T(256)S(1)}, s32[256]{0:T(256)}, u32[]{:S(2)}) copy-start(s32[256]{0:T(256)} %delay_hbm.1) | copy-start | bytes 3076

commit v2 on v1

--- a/solution.py
+++ b/solution.py
@@ -334,7 +334,7 @@
             sem,
         ],
         compiler_params=pltpu.CompilerParams(
-            collective_id=0, has_side_effects=True, vmem_limit_bytes=48 * 2**20
+            collective_id=0, has_side_effects=True, vmem_limit_bytes=67_043_328
         ),
     )(estimate, observed, delays, thresholds, table, cn)
 

time: 64.3 us -> 59.7 us (0.928)
  local copies, waits for them, and re-layouts: 7.46 us -> 2.82 us
    unnamed x14 -> x4, local copies, waits for them, and re-layouts: 7.46 us -> 2.82 us
where the time goes in v2:
time: 59.7 us; the launch traced here: 59.5 us
  Pallas kernels  56 us (94%)
  local copies, waits for them, and re-layouts  2.82 us (5%)
  between operations  0.65 us (1%)
    pallas_call x1, Pallas kernels, local(): pl.pallas_call(functools.partial(kernel, dims), out_shape=(jax.ShapeDtype...  56 us
    unnamed x4, local copies, waits for them, and re-layouts  2.82 us

profile of v2, /device:TPU:1, one launch (start us, length us, event | category | flops | bytes accessed | tf_op | source)
XLA Modules:
  0.0 59.5 jit_solution(1396751365682306847)
XLA Ops:
  0.6 56.0 %shard_map.77 = (f32[2,128,1024]{2,1,0:T(8,128)}, f32[2]{0:T(128)}) custom-call(bf16[2,128,1024]{2,1,0:T(8,128)(2,1)} %est_hbm.1, bf16[2,128,1024]{2,1,0:T(8,128)(2,1)} %obs_hbm.1, s32[256]{0:T(256)} %delay_hbm.1, f32[512]{0:T(512)} %level_hbm.1, bf16[1024,1024]{1,0:T(8,128)(2,1)} %constant.4.clone.table_hbm, bf16[512,256]{1,0:T(8,128)(2,1)} %constant.5.clone.cn_hbm), custom_call_target="tpu_custom_call" | custom-call | tf_op jit(solution)/shard_map/pallas_call | solution.py:296
  56.7 0.0 copy-start
  56.7 2.3 %copy.10 = f32[2,128,1024]{2,1,0:T(8,128)} copy(f32[2,128,1024]{2,1,0:T(8,128)} %get-tuple-element.4) | data formatting | bytes 2097152
  59.0 0.0 copy-done
  59.0 0.5 copy.11
Async XLA Ops:
  56.7 2.3 %copy-start = (f32[2]{0:T(128)S(1)}, f32[2]{0:T(128)}, u32[]{:S(2)}) copy-start(f32[2]{0:T(128)} %get-tuple-element.5) | copy-start | bytes 28

commit v3 on v1

--- a/solution.py
+++ b/solution.py
@@ -32,25 +32,26 @@
 
 def shift_left(x, lane, offset):
     length = x.shape[1]
-    return jnp.where(lane < length - offset, pltpu.roll(x, length - offset, 1), 0.0)
+    return jnp.where(lane < length - offset, pltpu.roll(x, (2 * length - offset) % length, 1), 0.0)
 
 
 def shift_right(x, lane, offset):
-    return jnp.where(lane >= offset, pltpu.roll(x, offset, 1), 0.0)
+    return jnp.where(lane >= offset, pltpu.roll(x, offset % x.shape[1], 1), 0.0)
 
 
 def kernel(
     dims,
     est_hbm, obs_hbm, delay_hbm, level_hbm, table_hbm, cn_hbm,
-    out_hbm, misfit_ref,
+    out, total,
     est, obs, delay, level, table, cn,
-    halo_out, halo_in, partial, stepped, energy, energies,
-    send1, recv1, wide1, wide2, send2, recv2, out,
-    load_sem, store_sem, halo_send, halo_recv, plane_sem,
+    halo_out, halo_in, est_in, partial, base, stepped, energy, energies,
+    send1, recv1, wide1, wide2, send2, recv2,
+    load_sem, halo_send, halo_recv, est_send, est_recv, plane_sem,
     send1_sem, recv1_sem, send2_sem, recv2_sem, energy_send, energy_recv,
 ):
     patches, n, rings, ring = dims
     shots, receivers, length = est.shape
+    rest = length - LONGEST
     bands = wide1.shape[0] // n // 4
     me, x = lax.axis_index("shot"), lax.axis_index("patch")
     z, place = me // ring, me % ring
@@ -88,14 +89,12 @@
 
     loads[0].wait()
     first = me * shots
-    d_before = delay[jnp.maximum(first - 1, 0)]
-    d_0 = delay[first]
-    d_1 = delay[first + 1]
-    d_after = delay[jnp.minimum(first + 2, last)]
-    a_before = SOURCE_SPACING + d_0 - d_before
-    a_here = SOURCE_SPACING + d_1 - d_0
-    a_after = SOURCE_SPACING + d_after - d_1
+    delays = [delay[jnp.clip(first + i, 0, last)] for i in range(-2, 4)]
+    a_prev, a_before, a_here, a_after, a_next = [SOURCE_SPACING + b - a for a, b in zip(delays, delays[1:])]
+    has_left = me > 0
+    has_right = me < n - 1
     lane = lax.broadcasted_iota(jnp.int32, (ROWS, length), 1)
+    lane_rest = lax.broadcasted_iota(jnp.int32, (ROWS, rest), 1)
     loads[1].wait()
     loads[2].wait()
 
@@ -107,10 +106,12 @@
         p1 = obs[1, rows, :].astype(jnp.float32) - e1 - shift_left(e0, lane, a_here)
         partial[0, rows, :] = p0
         partial[1, rows, :] = p1
-        halo_out[0, 0, rows, :] = shift_left(e1, lane, a_after)[:, :LONGEST].astype(jnp.bfloat16)
-        halo_out[0, 1, rows, :] = shift_left(p1, lane, a_after)[:, :LONGEST].astype(jnp.bfloat16)
-        halo_out[1, 0, rows, :] = shift_right(e0, lane, a_before)[:, length - LONGEST :].astype(jnp.bfloat16)
-        halo_out[1, 1, rows, :] = shift_right(p0, lane, a_before)[:, length - LONGEST :].astype(jnp.bfloat16)
+        once = shift_left(p1 - e1, lane, a_after)[:, :LONGEST]
+        twice = shift_left(e1[:, LONGEST:], lane_rest, a_after + a_next - LONGEST)
+        halo_out[0, rows, :] = jnp.concatenate([once, twice], axis=1).astype(jnp.bfloat16)
+        once = shift_right(p0 - e0, lane, a_before)[:, rest:]
+        twice = shift_right(e0[:, :rest], lane_rest, a_before + a_prev - LONGEST)
+        halo_out[1, rows, :] = jnp.concatenate([once, twice], axis=1).astype(jnp.bfloat16)
         return carry
 
     lax.fori_loop(0, receivers // ROWS, before_halo, 0)
@@ -124,7 +125,14 @@
         )
         for side, peer in enumerate([right, left])
     ]
-    for halo in halos:
+    raw_halos = [
+        pltpu.make_async_remote_copy(
+            est.at[1 - side, :, pl.ds(rest * (1 - side), LONGEST)], est_in.at[side], est_send.at[side], est_recv.at[side],
+            device_id={"shot": peer}, device_id_type=MESH,
+        )
+        for side, peer in enumerate([right, left])
+    ]
+    for halo in halos + raw_halos:
         halo.start()
 
     def plane_ready(i, carry):
@@ -132,6 +140,20 @@
         return carry
 
     lax.fori_loop(1, rings, plane_ready, 0)
+
+    def own_part(i, carry):
+        rows = pl.ds(i * ROWS, ROWS)
+        e0 = est[0, rows, :].astype(jnp.float32)
+        e1 = est[1, rows, :].astype(jnp.float32)
+        p0 = partial[0, rows, :]
+        p1 = partial[1, rows, :]
+        own0 = jnp.where(lane < jnp.where(has_left, length - a_before, 0), e0, 0.0)
+        own1 = jnp.where(lane >= jnp.where(has_right, a_after, length), e1, 0.0)
+        base[0, rows, :] = e0 + 0.5 * (p0 + shift_right(p1, lane, a_here) - own0)
+        base[1, rows, :] = e1 + 0.5 * (p1 + shift_left(p0, lane, a_here) - own1)
+        return carry
+
+    lax.fori_loop(0, receivers // ROWS, own_part, 0)
     for load in loads[3:]:
         load.wait()
     for halo in halos:
@@ -139,43 +161,15 @@
 
     def after_halo(i, carry):
         rows = pl.ds(i * ROWS, ROWS)
-        e0 = est[0, rows, :].astype(jnp.float32)
-        e1 = est[1, rows, :].astype(jnp.float32)
-        blank = jnp.zeros((ROWS, length - LONGEST), jnp.float32)
-        has_left = me > 0
-        has_right = me < n - 1
-
-        def from_left(kind):
-            got = halo_in[0, kind, rows, :].astype(jnp.float32)
-            return jnp.concatenate([jnp.where(has_left, got, 0.0), blank], axis=1)
-
-        def from_right(kind):
-            got = halo_in[1, kind, rows, :].astype(jnp.float32)
-            return jnp.concatenate([blank, jnp.where(has_right, got, 0.0)], axis=1)
-
-        r0 = partial[0, rows, :] - from_left(0)
-        r1 = partial[1, rows, :] - from_right(0)
-        own0 = jnp.where(lane < jnp.where(has_left, length - a_before, 0), e0, 0.0)
-        own1 = jnp.where(lane >= jnp.where(has_right, a_after, length), e1, 0.0)
-        s0 = e0 + 0.5 * (r0 + shift_right(r1, lane, a_here) + (from_left(1) - own0))
-        s1 = e1 + 0.5 * (r1 + shift_left(r0, lane, a_here) + (from_right(1) - own1))
-        stepped[rows, :] = s0.astype(jnp.bfloat16)
-        stepped[pl.ds(receivers + i * ROWS, ROWS), :] = s1.astype(jnp.bfloat16)
-
-        def squares(r):
-            total = jnp.zeros((8, 128), jnp.float32)
-            for a in range(0, ROWS, 8):
-                for b in range(0, length, 128):
-                    piece = r[a : a + 8, b : b + 128]
-                    total = total + piece * piece
-            return total
-
-        return carry[0] + squares(r0), carry[1] + squares(r1)
-
-    zero = jnp.zeros((8, 128), jnp.float32)
-    e_0, e_1 = lax.fori_loop(0, receivers // ROWS, after_halo, (zero, zero))
-    energy[0] = e_0
-    energy[1] = e_1
+        from_left = jnp.where(has_left, halo_in[0, rows, :].astype(jnp.float32), 0.0)
+        from_right = jnp.where(has_right, halo_in[1, rows, :].astype(jnp.float32), 0.0)
+        h0 = jnp.concatenate([from_left[:, :LONGEST], -from_right[:, LONGEST:]], axis=1)
+        h1 = jnp.concatenate([-from_left[:, LONGEST:], from_right[:, :LONGEST]], axis=1)
+        stepped[rows, :] = (base[0, rows, :] + 0.5 * h0).astype(jnp.bfloat16)
+        stepped[pl.ds(receivers + i * ROWS, ROWS), :] = (base[1, rows, :] + 0.5 * h1).astype(jnp.bfloat16)
+        return carry
+
+    lax.fori_loop(0, receivers // ROWS, after_halo, 0)
 
     pl.semaphore_wait(plane_sem, rings - 1)
 
@@ -215,6 +209,31 @@
         planes(offsets)
         send_planes(offsets, lambda d: send1.at[d], lambda d: recv1.at[d], send1_sem, recv1_sem)
 
+    for halo in raw_halos:
+        halo.wait_recv()
+
+    def misfit_part(i, carry):
+        rows = pl.ds(i * ROWS, ROWS)
+        blank = jnp.zeros((ROWS, rest), jnp.float32)
+        from_left = jnp.concatenate([blank, est_in[0, rows, :].astype(jnp.float32)], axis=1)
+        from_right = jnp.concatenate([est_in[1, rows, :].astype(jnp.float32), blank], axis=1)
+        r0 = partial[0, rows, :] - jnp.where(has_left, shift_left(from_left, lane, a_before), 0.0)
+        r1 = partial[1, rows, :] - jnp.where(has_right, shift_right(from_right, lane, a_after), 0.0)
+
+        def squares(r):
+            parts = jnp.zeros((8, 128), jnp.float32)
+            for a in range(0, ROWS, 8):
+                for b in range(0, length, 128):
+                    piece = r[a : a + 8, b : b + 128]
+                    parts = parts + piece * piece
+            return parts
+
+        return carry[0] + squares(r0), carry[1] + squares(r1)
+
+    zero = jnp.zeros((8, 128), jnp.float32)
+    e_0, e_1 = lax.fori_loop(0, receivers // ROWS, misfit_part, (zero, zero))
+    energy[0] = e_0
+    energy[1] = e_1
     for i in range(1, patches):
         pltpu.make_async_remote_copy(
             energy, energies.at[x], energy_send.at[i], energy_recv,
@@ -255,33 +274,36 @@
         send_planes(offsets, lambda d: send2.at[:, d], lambda d: recv2.at[:, d], send2_sem, recv2_sem)
 
     pltpu.make_async_copy(energies, energies, energy_recv).wait()
-    total = energies[0]
-    for i in range(1, patches):
-        total = total + energies[i]
-    for s in range(shots):
-        misfit_ref[s] = jnp.sum(total[s]) / (patches * receivers * length)
-
-    pltpu.make_async_copy(recv2, recv2, recv2_sem).wait()
-
-    stores = []
-    for s in range(shots):
-        field = recv2[s].astype(jnp.float32).reshape(n * 8, receivers).astype(jnp.bfloat16)
-        out[s] = lax.dot_general(field, table[...], (((0,), (0,)), ((), ())), preferred_element_type=jnp.float32)
-        stores.append(pltpu.make_async_copy(out.at[s], out_hbm.at[s], store_sem.at[s]))
-        stores[-1].start()
-
-    for halo in halos:
+    total[...] = sum(energies[i] for i in range(patches))
+
+    for halo in halos + raw_halos:
         halo.wait_send()
     for i in range(1, patches):
         pltpu.make_async_remote_copy(
             energy, energies.at[x], energy_send.at[i], energy_recv,
             device_id={"patch": (x + i) % patches}, device_id_type=MESH,
         ).wait_send()
-    rest = pl.ds(0, n - 1)
-    pltpu.make_async_copy(send1.at[rest], send1.at[rest], send1_sem).wait()
-    pltpu.make_async_copy(send2.at[:, rest], send2.at[:, rest], send2_sem).wait()
-    for store in stores:
-        store.wait()
+    others = pl.ds(0, n - 1)
+    pltpu.make_async_copy(send1.at[others], send1.at[others], send1_sem).wait()
+
+    pltpu.make_async_copy(recv2, recv2, recv2_sem).wait()
+
+    for s in range(shots):
+        field = recv2[s].astype(jnp.float32).reshape(n * 8, receivers).astype(jnp.bfloat16)
+        out[s] = lax.dot_general(field, table[...], (((0,), (0,)), ((), ())), preferred_element_type=jnp.float32)
+
+    pltpu.make_async_copy(send2.at[:, others], send2.at[:, others], send2_sem).wait()
+
+
+def finish(count, field, total, out, misfit, sems):
+    shots = field.shape[0]
+    copies = [pltpu.make_async_copy(field.at[s], out.at[s], sems.at[s]) for s in range(shots)]
+    for copy in copies:
+        copy.start()
+    for s in range(shots):
+        misfit[s] = jnp.sum(total[s]) / count
+    for copy in copies:
+        copy.wait()
 
 
 def local(dims, estimate, observed, delays, thresholds):
@@ -293,14 +315,16 @@
     cn = jnp.asarray(shot_table(n * shots, shots))
     bands = frequencies // n
     sem = pltpu.SemaphoreType.DMA
-    return pl.pallas_call(
+    vmem = pl.BlockSpec(memory_space=pltpu.VMEM)
+    operands = (estimate, observed, delays, thresholds, table, cn)
+    field, total = pl.pallas_call(
         functools.partial(kernel, dims),
         out_shape=(
             jax.ShapeDtypeStruct((shots, receivers, length), f32),
-            jax.ShapeDtypeStruct((shots,), f32),
+            jax.ShapeDtypeStruct((shots, 8, 128), f32),
         ),
-        in_specs=[pl.BlockSpec(memory_space=pl.ANY)] * 6,
-        out_specs=(pl.BlockSpec(memory_space=pl.ANY), pl.BlockSpec(memory_space=pltpu.SMEM)),
+        in_specs=[pl.BlockSpec(memory_space=pltpu.HBM)] * 6,
+        out_specs=(vmem, vmem),
         scratch_shapes=[
             pltpu.VMEM(estimate.shape, bf16),
             pltpu.VMEM(estimate.shape, bf16),
@@ -308,8 +332,10 @@
             pltpu.SMEM(thresholds.shape, f32),
             pltpu.VMEM(table.shape, bf16),
             pltpu.VMEM(cn.shape, bf16),
-            pltpu.VMEM((2, 2, receivers, LONGEST), bf16),
-            pltpu.VMEM((2, 2, receivers, LONGEST), bf16),
+            pltpu.VMEM((2, receivers, length), bf16),
+            pltpu.VMEM((2, receivers, length), bf16),
+            pltpu.VMEM((2, receivers, LONGEST), bf16),
+            pltpu.VMEM(estimate.shape, f32),
             pltpu.VMEM(estimate.shape, f32),
             pltpu.VMEM((shots * receivers, length), bf16),
             pltpu.VMEM((shots, 8, 128), f32),
@@ -320,9 +346,9 @@
             pltpu.VMEM((n * 4 * bands, receivers), f32),
             pltpu.VMEM((shots, n, 8, receivers), bf16),
             pltpu.VMEM((shots, n, 8, receivers), bf16),
-            pltpu.VMEM(estimate.shape, f32),
             sem((6,)),
-            sem((shots,)),
+            sem((2,)),
+            sem((2,)),
             sem((2,)),
             sem((2,)),
             pltpu.SemaphoreType.REGULAR,
@@ -336,7 +362,15 @@
         compiler_params=pltpu.CompilerParams(
             collective_id=0, has_side_effects=True, vmem_limit_bytes=48 * 2**20
         ),
-    )(estimate, observed, delays, thresholds, table, cn)
+    )(*[pltpu.with_memory_space_constraint(v, pltpu.HBM) for v in operands])
+    return pl.pallas_call(
+        functools.partial(finish, dims[0] * receivers * length),
+        out_shape=(jax.ShapeDtypeStruct(field.shape, f32), jax.ShapeDtypeStruct((shots,), f32)),
+        in_specs=[vmem, vmem],
+        out_specs=(pl.BlockSpec(memory_space=pltpu.HBM), pl.BlockSpec(memory_space=pltpu.SMEM)),
+        scratch_shapes=[sem((shots,))],
+        compiler_params=pltpu.CompilerParams(vmem_limit_bytes=8 * 2**20),
+    )(field, total)
 
 
 def solution(mesh):

time: 64.3 us -> 54.5 us (0.85)
  local copies, waits for them, and re-layouts: 7.46 us -> 0 us
  Pallas kernels: 55.9 us -> 53.8 us
    unnamed x14 -> x0, local copies, waits for them, and re-layouts: 7.46 us -> none
    pallas_call x1, Pallas kernels: 55.9 us -> 52.3 us  [local(): pl.pallas_call(functools.partial(kernel, dims), out_shape=(jax.ShapeDtype...]
    pallas_call x0 -> x1, Pallas kernels: none -> 1.5 us  [local(): pl.pallas_call(functools.partial(finish, dims[0] * receivers * length), o...]
where the time goes in v3:
time: 54.5 us; the launch traced here: 54.4 us
  Pallas kernels  53.8 us (99%)
  between operations  0.64 us (1%)
    pallas_call x1, Pallas kernels, local(): pl.pallas_call(functools.partial(kernel, dims), out_shape=(jax.ShapeDtype...  52.3 us
    pallas_call x1, Pallas kernels, local(): pl.pallas_call(functools.partial(finish, dims[0] * receivers * length), o...  1.5 us

profile of v3, /device:TPU:1, one launch (start us, length us, event | category | flops | bytes accessed | tf_op | source)
XLA Modules:
  0.0 54.4 jit_solution(10501704890875584289)
XLA Ops:
  0.6 52.3 %shard_map.77 = (f32[2,128,1024]{2,1,0:T(8,128)S(1)}, f32[2,8,128]{2,1,0:T(8,128)S(1)}) custom-call(bf16[2,128,1024]{2,1,0:T(8,128)(2,1)} %est_hbm.1, bf16[2,128,1024]{2,1,0:T(8,128)(2,1)} %obs_hbm.1, s32[256]{0:T(256)} %delay_hbm.1, f32[512]{0:T(512)} %level_hbm.1, bf16[1024,1024]{1,0:T(8,128)(2,1)} %constant.4.clone.table_hbm, ...), custom_call_target="tpu_custom_call" | custom-call | tf_op jit(solution)/shard_map/pallas_call | solution.py:320
  52.9 1.5 %shard_map.78 = (f32[2,128,1024]{2,1,0:T(8,128)}, f32[2]{0:T(128)}) custom-call(f32[2,128,1024]{2,1,0:T(8,128)S(1)} %get-tuple-element.4.field, f32[2,8,128]{2,1,0:T(8,128)S(1)} %get-tuple-element.5.total), custom_call_target="tpu_custom_call" | custom-call | tf_op jit(solution)/shard_map/pallas_call | solution.py:366

commit v4 on v3

--- a/solution.py
+++ b/solution.py
@@ -16,10 +16,11 @@
 MESH = pl.DeviceIdType.MESH
 
 
-def time_table(frequencies, samples):
+def time_table(frequencies, samples, n, halves):
     phase = np.arange(frequencies)[:, None] * np.arange(samples)[None, :] % samples
     angle = 2.0 * math.pi * phase / samples
     table = np.stack([np.cos(angle), -np.sin(angle)], axis=1) / math.sqrt(samples)
+    table = table.reshape(n, halves, -1, samples).swapaxes(0, 1)
     return table.reshape(2 * frequencies, samples).astype(np.float32).astype(ml_dtypes.bfloat16)
 
 
@@ -52,7 +53,8 @@
     patches, n, rings, ring = dims
     shots, receivers, length = est.shape
     rest = length - LONGEST
-    bands = wide1.shape[0] // n // 4
+    halves = wide1.shape[0]
+    bands = 2 * halves
     me, x = lax.axis_index("shot"), lax.axis_index("patch")
     z, place = me // ring, me % ring
     right, left = (me + 1) % n, (me + n - 1) % n
@@ -173,14 +175,20 @@
 
     pl.semaphore_wait(plane_sem, rings - 1)
 
-    def planes(offsets):
+    upper = lax.broadcasted_iota(jnp.int32, (ring // 2, 8, receivers), 1) < 4
+
+    def planes(h, offsets):
         field = stepped[...]
-        for dz in offsets:
-            zz = (z + dz) % rings
-            rows = table[pl.ds(pl.multiple_of(zz * (ring * 8), ring * 8), ring * 8), :]
-            got = lax.dot_general(rows, field, (((1,), (1,)), ((), ())), preferred_element_type=jnp.float32)
-            tiles = [got[:, s * receivers : (s + 1) * receivers].reshape(ring, 8, receivers) for s in range(shots)]
-            send1[pl.ds(zz * ring, ring)] = jnp.concatenate(tiles, axis=1).astype(jnp.bfloat16)
+        starts = [pl.multiple_of((h * n + (z + dz) % rings * ring) * 4, 4 * ring) for dz in offsets]
+        rows = jnp.concatenate([table[pl.ds(start, 4 * ring), :] for start in starts], axis=0)
+        got = lax.dot_general(rows, field, (((1,), (1,)), ((), ())), preferred_element_type=jnp.float32)
+        for j, dz in enumerate(offsets):
+            pairs = got[j * 4 * ring : (j + 1) * 4 * ring].reshape(ring // 2, 8, shots * receivers)
+            g0, g1 = pairs[:, :, :receivers], pairs[:, :, receivers:]
+            even = jnp.where(upper, g0, pltpu.roll(g1, 4, 1))
+            odd = jnp.where(upper, pltpu.roll(g0, 4, 1), g1)
+            tiles = jnp.stack([even, odd], axis=1).reshape(ring, 8, receivers)
+            send1[h, pl.ds((z + dz) % rings * ring, ring)] = tiles.astype(jnp.bfloat16)
 
     def send_planes(offsets, src, dst, ssem, rsem):
         def one(i, carry):
@@ -205,9 +213,10 @@
 
     half = rings // 2
     groups = [(half, 0)] + [(dz, rings - dz) for dz in range(half - 1, 0, -1)]
-    for offsets in groups:
-        planes(offsets)
-        send_planes(offsets, lambda d: send1.at[d], lambda d: recv1.at[d], send1_sem, recv1_sem)
+    for h in range(halves):
+        for offsets in groups:
+            planes(h, offsets)
+            send_planes(offsets, lambda d: send1.at[h, d], lambda d: recv1.at[h, d], send1_sem.at[h], recv1_sem.at[h])
 
     for halo in raw_halos:
         halo.wait_recv()
@@ -241,37 +250,40 @@
         ).start()
     pltpu.make_async_copy(energy, energies.at[x], energy_recv).start()
 
-    pltpu.make_async_copy(recv1, recv1, recv1_sem).wait()
-
-    wide1[...] = recv1[...].astype(jnp.float32).reshape(wide1.shape)
     wave = cn[...]
     k = n * shots
-    for band in range(bands):
-        columns = []
-        for q in range(2):
-            parts = [wide1[pl.ds(s * 8 + band * 2 + q, n, stride=16), :] for s in range(shots)]
-            columns.append(jnp.concatenate(parts, axis=0))
-        field = jnp.concatenate(columns, axis=1).astype(jnp.bfloat16)
-        got = jnp.dot(wave, field, preferred_element_type=jnp.float32)
-        real = got[:k, :receivers] + got[k:, receivers:]
-        imag = got[:k, receivers:] - got[k:, :receivers]
-        f = me * bands + band
-        limit = level[f]
-        weight = jnp.where(f == 0, 1.0, 2.0)
-        magnitude = jnp.sqrt(real * real + imag * imag)
-        factor = jnp.maximum(magnitude - limit, 0.0) / jnp.maximum(magnitude, limit) * weight
-        shrunk = jnp.concatenate([real * factor, imag * factor], axis=1).astype(jnp.bfloat16)
-        got = jnp.dot(wave, shrunk, preferred_element_type=jnp.float32)
-        real = got[:k, :receivers] - got[k:, receivers:]
-        imag = got[:k, receivers:] + got[k:, :receivers]
-        for s in range(shots):
-            wide2[pl.ds(s * 8 + band * 2, n, stride=16), :] = real[s * n : (s + 1) * n]
-            wide2[pl.ds(s * 8 + band * 2 + 1, n, stride=16), :] = imag[s * n : (s + 1) * n]
-    tiles = wide2[...].reshape(n, 16, receivers)
-    for s in range(shots):
-        send2[s] = tiles[:, s * 8 : (s + 1) * 8, :].astype(jnp.bfloat16)
-    for offsets in groups:
-        send_planes(offsets, lambda d: send2.at[:, d], lambda d: recv2.at[:, d], send2_sem, recv2_sem)
+
+    def shrink(h):
+        w1, w2 = wide1.at[h], wide2.at[h]
+        w1[...] = recv1[h].astype(jnp.float32).reshape(8 * n, receivers)
+        for b in range(bands // halves):
+            columns = []
+            for q in range(2):
+                parts = [w1[pl.ds(s * 4 + b * 2 + q, n, stride=8), :] for s in range(shots)]
+                columns.append(jnp.concatenate(parts, axis=0))
+            field = jnp.concatenate(columns, axis=1).astype(jnp.bfloat16)
+            got = jnp.dot(wave, field, preferred_element_type=jnp.float32)
+            real = got[:k, :receivers] + got[k:, receivers:]
+            imag = got[:k, receivers:] - got[k:, :receivers]
+            f = me * bands + h * (bands // halves) + b
+            limit = level[f]
+            weight = jnp.where(f == 0, 1.0, 2.0)
+            magnitude = jnp.sqrt(real * real + imag * imag)
+            factor = jnp.maximum(magnitude - limit, 0.0) / jnp.maximum(magnitude, limit) * weight
+            shrunk = jnp.concatenate([real * factor, imag * factor], axis=1).astype(jnp.bfloat16)
+            got = jnp.dot(wave, shrunk, preferred_element_type=jnp.float32)
+            real = got[:k, :receivers] - got[k:, receivers:]
+            imag = got[:k, receivers:] + got[k:, :receivers]
+            for s in range(shots):
+                w2[pl.ds(s * 4 + b * 2, n, stride=8), :] = real[s * n : (s + 1) * n]
+                w2[pl.ds(s * 4 + b * 2 + 1, n, stride=8), :] = imag[s * n : (s + 1) * n]
+        send2[h] = w2[...].reshape(n, 8, receivers).astype(jnp.bfloat16)
+
+    for h in range(halves):
+        pltpu.make_async_copy(recv1.at[h], recv1.at[h], recv1_sem.at[h]).wait()
+        shrink(h)
+        for offsets in groups:
+            send_planes(offsets, lambda d: send2.at[h, d], lambda d: recv2.at[h, d], send2_sem.at[h], recv2_sem.at[h])
 
     pltpu.make_async_copy(energies, energies, energy_recv).wait()
     total[...] = sum(energies[i] for i in range(patches))
@@ -284,15 +296,26 @@
             device_id={"patch": (x + i) % patches}, device_id_type=MESH,
         ).wait_send()
     others = pl.ds(0, n - 1)
-    pltpu.make_async_copy(send1.at[others], send1.at[others], send1_sem).wait()
-
-    pltpu.make_async_copy(recv2, recv2, recv2_sem).wait()
-
-    for s in range(shots):
-        field = recv2[s].astype(jnp.float32).reshape(n * 8, receivers).astype(jnp.bfloat16)
-        out[s] = lax.dot_general(field, table[...], (((0,), (0,)), ((), ())), preferred_element_type=jnp.float32)
-
-    pltpu.make_async_copy(send2.at[:, others], send2.at[:, others], send2_sem).wait()
+    for h in range(halves):
+        pltpu.make_async_copy(send1.at[h, others], send1.at[h, others], send1_sem.at[h]).wait()
+
+    first_rows = lax.broadcasted_iota(jnp.int32, (n // 2, 8, receivers), 1) < 4
+    for h in range(halves):
+        pltpu.make_async_copy(recv2.at[h], recv2.at[h], recv2_sem.at[h]).wait()
+        pairs = recv2[h].astype(jnp.float32).reshape(n // 2, 2, 8, receivers)
+        even, odd = pairs[:, 0], pairs[:, 1]
+        fields = [
+            jnp.where(first_rows, even, pltpu.roll(odd, 4, 1)),
+            jnp.where(first_rows, pltpu.roll(even, 4, 1), odd),
+        ]
+        rows = table[h * 4 * n : (h + 1) * 4 * n, :]
+        for s in range(shots):
+            field = fields[s].reshape(4 * n, receivers).astype(jnp.bfloat16)
+            got = lax.dot_general(field, rows, (((0,), (0,)), ((), ())), preferred_element_type=jnp.float32)
+            out[s] = got if h == 0 else out[s] + got
+
+    for h in range(halves):
+        pltpu.make_async_copy(send2.at[h, others], send2.at[h, others], send2_sem.at[h]).wait()
 
 
 def finish(count, field, total, out, misfit, sems):
@@ -311,9 +334,10 @@
     n = dims[1]
     frequencies = thresholds.shape[0]
     bf16, f32 = jnp.bfloat16, jnp.float32
-    table = jnp.asarray(time_table(frequencies, length))
+    bands = frequencies // n
+    halves = bands // 2
+    table = jnp.asarray(time_table(frequencies, length, n, halves))
     cn = jnp.asarray(shot_table(n * shots, shots))
-    bands = frequencies // n
     sem = pltpu.SemaphoreType.DMA
     vmem = pl.BlockSpec(memory_space=pltpu.VMEM)
     operands = (estimate, observed, delays, thresholds, table, cn)
@@ -340,22 +364,22 @@
             pltpu.VMEM((shots * receivers, length), bf16),
             pltpu.VMEM((shots, 8, 128), f32),
             pltpu.VMEM((dims[0], shots, 8, 128), f32),
-            pltpu.VMEM((n, 16, receivers), bf16),
-            pltpu.VMEM((n, 16, receivers), bf16),
-            pltpu.VMEM((n * 4 * bands, receivers), f32),
-            pltpu.VMEM((n * 4 * bands, receivers), f32),
-            pltpu.VMEM((shots, n, 8, receivers), bf16),
-            pltpu.VMEM((shots, n, 8, receivers), bf16),
+            pltpu.VMEM((halves, n, 8, receivers), bf16),
+            pltpu.VMEM((halves, n, 8, receivers), bf16),
+            pltpu.VMEM((halves, n * 8, receivers), f32),
+            pltpu.VMEM((halves, n * 8, receivers), f32),
+            pltpu.VMEM((halves, n, 8, receivers), bf16),
+            pltpu.VMEM((halves, n, 8, receivers), bf16),
             sem((6,)),
             sem((2,)),
             sem((2,)),
             sem((2,)),
             sem((2,)),
             pltpu.SemaphoreType.REGULAR,
-            sem,
-            sem,
-            sem,
-            sem,
+            sem((halves,)),
+            sem((halves,)),
+            sem((halves,)),
+            sem((halves,)),
             sem((dims[0],)),
             sem,
         ],

time: 54.5 us -> 51.2 us (0.939)
  Pallas kernels: 53.8 us -> 50.4 us
    pallas_call x1, Pallas kernels: 52.3 us -> 48.9 us  [local(): pl.pallas_call(functools.partial(kernel, dims), out_shape=(jax.ShapeDtype...]
where the time goes in v4:
time: 51.2 us; the launch traced here: 51 us
  Pallas kernels  50.4 us (98%)
  between operations  0.64 us (1%)
    pallas_call x1, Pallas kernels, local(): pl.pallas_call(functools.partial(kernel, dims), out_shape=(jax.ShapeDtype...  48.9 us
    pallas_call x1, Pallas kernels, local(): pl.pallas_call(functools.partial(finish, dims[0] * receivers * length), o...  1.5 us

profile of v4, /device:TPU:1, one launch (start us, length us, event | category | flops | bytes accessed | tf_op | source)
XLA Modules:
  0.0 51.0 jit_solution(4568287626196456316)
XLA Ops:
  0.6 48.9 %shard_map.77 = (f32[2,128,1024]{2,1,0:T(8,128)S(1)}, f32[2,8,128]{2,1,0:T(8,128)S(1)}) custom-call(bf16[2,128,1024]{2,1,0:T(8,128)(2,1)} %est_hbm.1, bf16[2,128,1024]{2,1,0:T(8,128)(2,1)} %obs_hbm.1, s32[256]{0:T(256)} %delay_hbm.1, f32[512]{0:T(512)} %level_hbm.1, bf16[1024,1024]{1,0:T(8,128)(2,1)} %constant.4.clone.table_hbm, ...), custom_call_target="tpu_custom_call" | custom-call | tf_op jit(solution)/shard_map/pallas_call | solution.py:344
  49.5 1.5 %shard_map.78 = (f32[2,128,1024]{2,1,0:T(8,128)}, f32[2]{0:T(128)}) custom-call(f32[2,128,1024]{2,1,0:T(8,128)S(1)} %get-tuple-element.4.field, f32[2,8,128]{2,1,0:T(8,128)S(1)} %get-tuple-element.5.total), custom_call_target="tpu_custom_call" | custom-call | tf_op jit(solution)/shard_map/pallas_call | solution.py:390

commit v5 on v4

--- a/solution.py
+++ b/solution.py
@@ -13,6 +13,7 @@
 SOURCE_SPACING = 512
 LONGEST = 768
 ROWS = 16
+BLOCKS = 4
 MESH = pl.DeviceIdType.MESH
 
 
@@ -47,7 +48,7 @@
     est, obs, delay, level, table, cn,
     halo_out, halo_in, est_in, partial, base, stepped, energy, energies,
     send1, recv1, wide1, wide2, send2, recv2,
-    load_sem, halo_send, halo_recv, est_send, est_recv, plane_sem,
+    load_sem, record_sem, halo_send, halo_recv, est_send, est_recv, plane_sem,
     send1_sem, recv1_sem, send2_sem, recv2_sem, energy_send, energy_recv,
 ):
     patches, n, rings, ring = dims
@@ -62,11 +63,21 @@
 
     loads = [
         pltpu.make_async_copy(src, dst, load_sem.at[i])
-        for i, (src, dst) in enumerate(
-            [(delay_hbm, delay), (est_hbm, est), (obs_hbm, obs), (level_hbm, level), (table_hbm, table), (cn_hbm, cn)]
-        )
+        for i, (src, dst) in enumerate([(delay_hbm, delay), (level_hbm, level), (table_hbm, table), (cn_hbm, cn)])
     ]
-    for load in loads:
+
+    def record_loads(block):
+        rows = pl.ds(block * (receivers // BLOCKS), receivers // BLOCKS)
+        return [
+            pltpu.make_async_copy(src.at[:, rows], dst.at[:, rows], record_sem.at[i, block])
+            for i, (src, dst) in enumerate([(est_hbm, est), (obs_hbm, obs)])
+        ]
+
+    loads[0].start()
+    for block in range(BLOCKS):
+        for load in record_loads(block):
+            load.start()
+    for load in loads[1:]:
         load.start()
 
     barrier = pltpu.get_barrier_semaphore()
@@ -97,8 +108,6 @@
     has_right = me < n - 1
     lane = lax.broadcasted_iota(jnp.int32, (ROWS, length), 1)
     lane_rest = lax.broadcasted_iota(jnp.int32, (ROWS, rest), 1)
-    loads[1].wait()
-    loads[2].wait()
 
     def before_halo(i, carry):
         rows = pl.ds(i * ROWS, ROWS)
@@ -116,17 +125,26 @@
         halo_out[1, rows, :] = jnp.concatenate([once, twice], axis=1).astype(jnp.bfloat16)
         return carry
 
-    lax.fori_loop(0, receivers // ROWS, before_halo, 0)
-
-    pl.semaphore_wait(barrier, ring - 1 + rings - 1 + patches - 1 + 2)
-
-    halos = [
-        pltpu.make_async_remote_copy(
-            halo_out.at[side], halo_in.at[side], halo_send.at[side], halo_recv.at[side],
-            device_id={"shot": peer}, device_id_type=MESH,
-        )
-        for side, peer in enumerate([right, left])
-    ]
+    def halo_copies(block):
+        rows = pl.ds(block * (receivers // BLOCKS), receivers // BLOCKS)
+        return [
+            pltpu.make_async_remote_copy(
+                halo_out.at[side, rows], halo_in.at[side, rows], halo_send.at[side, block], halo_recv.at[side, block],
+                device_id={"shot": peer}, device_id_type=MESH,
+            )
+            for side, peer in enumerate([right, left])
+        ]
+
+    steps = receivers // ROWS // BLOCKS
+    for block in range(BLOCKS):
+        for load in record_loads(block):
+            load.wait()
+        lax.fori_loop(block * steps, (block + 1) * steps, before_halo, 0)
+        if block == 0:
+            pl.semaphore_wait(barrier, ring - 1 + rings - 1 + patches - 1 + 2)
+        for halo in halo_copies(block):
+            halo.start()
+
     raw_halos = [
         pltpu.make_async_remote_copy(
             est.at[1 - side, :, pl.ds(rest * (1 - side), LONGEST)], est_in.at[side], est_send.at[side], est_recv.at[side],
@@ -134,7 +152,7 @@
         )
         for side, peer in enumerate([right, left])
     ]
-    for halo in halos + raw_halos:
+    for halo in raw_halos:
         halo.start()
 
     def plane_ready(i, carry):
@@ -156,10 +174,8 @@
         return carry
 
     lax.fori_loop(0, receivers // ROWS, own_part, 0)
-    for load in loads[3:]:
+    for load in loads[1:]:
         load.wait()
-    for halo in halos:
-        halo.wait_recv()
 
     def after_halo(i, carry):
         rows = pl.ds(i * ROWS, ROWS)
@@ -171,7 +187,10 @@
         stepped[pl.ds(receivers + i * ROWS, ROWS), :] = (base[1, rows, :] + 0.5 * h1).astype(jnp.bfloat16)
         return carry
 
-    lax.fori_loop(0, receivers // ROWS, after_halo, 0)
+    for block in range(BLOCKS):
+        for halo in halo_copies(block):
+            halo.wait_recv()
+        lax.fori_loop(block * steps, (block + 1) * steps, after_halo, 0)
 
     pl.semaphore_wait(plane_sem, rings - 1)
 
@@ -190,33 +209,38 @@
             tiles = jnp.stack([even, odd], axis=1).reshape(ring, 8, receivers)
             send1[h, pl.ds((z + dz) % rings * ring, ring)] = tiles.astype(jnp.bfloat16)
 
-    def send_planes(offsets, src, dst, ssem, rsem):
-        def one(i, carry):
-            for dz in offsets:
-                peer = (z + dz) % rings * ring + (place + i) % ring
+    def send_shell(hops, src, dst, ssem, rsem):
+        for far_z in range(half + 1):
+            far_y = hops - far_z
+            if not 0 <= far_y <= half:
+                continue
+            both_z, both_y = far_z % half > 0, far_y % half > 0
+
+            def one(i, carry):
+                dz, dy = far_z, far_y
+                rest_of = i // 2
+                if both_y:
+                    dy = far_y + lax.rem(rest_of, 2) * (rings - 2 * far_y)
+                    rest_of = rest_of // 2
+                if both_z:
+                    dz = far_z + rest_of * (rings - 2 * far_z)
+                peer = lax.rem(z + dz, rings) * ring + lax.rem(place // 2 + dy, rings) * 2 + lax.rem(place + i, 2)
                 pltpu.make_async_remote_copy(
                     src(peer), dst(me), ssem, rsem, device_id={"shot": peer}, device_id_type=MESH
                 ).start()
-            return carry
-
-        if 0 in offsets:
-            far = tuple(dz for dz in offsets if dz)
-            for dz in far:
-                peer = (z + dz) % rings * ring + place
-                pltpu.make_async_remote_copy(
-                    src(peer), dst(me), ssem, rsem, device_id={"shot": peer}, device_id_type=MESH
-                ).start()
-            pltpu.make_async_copy(src(me), dst(me), rsem).start()
-            lax.fori_loop(1, ring, one, 0)
-        else:
-            lax.fori_loop(0, ring, one, 0)
+                return carry
+
+            if hops == 0:
+                pltpu.make_async_copy(src(me), dst(me), rsem).start()
+            lax.fori_loop(1 if hops == 0 else 0, 2 * (1 + both_z) * (1 + both_y), one, 0)
 
     half = rings // 2
-    groups = [(half, 0)] + [(dz, rings - dz) for dz in range(half - 1, 0, -1)]
     for h in range(halves):
-        for offsets in groups:
-            planes(h, offsets)
-            send_planes(offsets, lambda d: send1.at[h, d], lambda d: recv1.at[h, d], send1_sem.at[h], recv1_sem.at[h])
+        for hops in range(2 * half, -1, -1):
+            near = hops - half
+            if near >= 0:
+                planes(h, sorted({near, (rings - near) % rings}))
+            send_shell(hops, lambda d: send1.at[h, d], lambda d: recv1.at[h, d], send1_sem.at[h], recv1_sem.at[h])
 
     for halo in raw_halos:
         halo.wait_recv()
@@ -282,13 +306,16 @@
     for h in range(halves):
         pltpu.make_async_copy(recv1.at[h], recv1.at[h], recv1_sem.at[h]).wait()
         shrink(h)
-        for offsets in groups:
-            send_planes(offsets, lambda d: send2.at[h, d], lambda d: recv2.at[h, d], send2_sem.at[h], recv2_sem.at[h])
+        for hops in range(2 * half, -1, -1):
+            send_shell(hops, lambda d: send2.at[h, d], lambda d: recv2.at[h, d], send2_sem.at[h], recv2_sem.at[h])
 
     pltpu.make_async_copy(energies, energies, energy_recv).wait()
     total[...] = sum(energies[i] for i in range(patches))
 
-    for halo in halos + raw_halos:
+    for block in range(BLOCKS):
+        for halo in halo_copies(block):
+            halo.wait_send()
+    for halo in raw_halos:
         halo.wait_send()
     for i in range(1, patches):
         pltpu.make_async_remote_copy(
@@ -318,13 +345,15 @@
         pltpu.make_async_copy(send2.at[h, others], send2.at[h, others], send2_sem.at[h]).wait()
 
 
-def finish(count, field, total, out, misfit, sems):
+def finish(count, field, total, out, misfit, means, sems):
     shots = field.shape[0]
     copies = [pltpu.make_async_copy(field.at[s], out.at[s], sems.at[s]) for s in range(shots)]
     for copy in copies:
         copy.start()
     for s in range(shots):
-        misfit[s] = jnp.sum(total[s]) / count
+        means[s] = jnp.sum(total[s]) / count
+    copies.append(pltpu.make_async_copy(means, misfit, sems.at[shots]))
+    copies[-1].start()
     for copy in copies:
         copy.wait()
 
@@ -370,9 +399,10 @@
             pltpu.VMEM((halves, n * 8, receivers), f32),
             pltpu.VMEM((halves, n, 8, receivers), bf16),
             pltpu.VMEM((halves, n, 8, receivers), bf16),
-            sem((6,)),
-            sem((2,)),
-            sem((2,)),
+            sem((4,)),
+            sem((2, BLOCKS)),
+            sem((2, BLOCKS)),
+            sem((2, BLOCKS)),
             sem((2,)),
             sem((2,)),
             pltpu.SemaphoreType.REGULAR,
@@ -391,8 +421,8 @@
         functools.partial(finish, dims[0] * receivers * length),
         out_shape=(jax.ShapeDtypeStruct(field.shape, f32), jax.ShapeDtypeStruct((shots,), f32)),
         in_specs=[vmem, vmem],
-        out_specs=(pl.BlockSpec(memory_space=pltpu.HBM), pl.BlockSpec(memory_space=pltpu.SMEM)),
-        scratch_shapes=[sem((shots,))],
+        out_specs=(pl.BlockSpec(memory_space=pltpu.HBM), pl.BlockSpec(memory_space=pltpu.HBM)),
+        scratch_shapes=[pltpu.SMEM((shots,), f32), sem((shots + 1,))],
         compiler_params=pltpu.CompilerParams(vmem_limit_bytes=8 * 2**20),
     )(field, total)
 

time: 51.2 us -> 52.6 us (1.027)
  Pallas kernels: 50.4 us -> 51.9 us
    pallas_call x1, Pallas kernels: 48.9 us -> 50.8 us  [local(): pl.pallas_call(functools.partial(kernel, dims), out_shape=(jax.ShapeDtype...]
where the time goes in v5:
time: 52.6 us; the launch traced here: 52.5 us
  Pallas kernels  51.9 us (99%)
  between operations  0.64 us (1%)
    pallas_call x1, Pallas kernels, local(): pl.pallas_call(functools.partial(kernel, dims), out_shape=(jax.ShapeDtype...  50.8 us

profile of v5, /device:TPU:1, one launch (start us, length us, event | category | flops | bytes accessed | tf_op | source)
XLA Modules:
  0.0 52.5 jit_solution(13804457022590979521)
XLA Ops:
  0.6 50.8 %shard_map.77 = (f32[2,128,1024]{2,1,0:T(8,128)S(1)}, f32[2,8,128]{2,1,0:T(8,128)S(1)}) custom-call(bf16[2,128,1024]{2,1,0:T(8,128)(2,1)} %est_hbm.1, bf16[2,128,1024]{2,1,0:T(8,128)(2,1)} %obs_hbm.1, s32[256]{0:T(256)} %delay_hbm.1, f32[512]{0:T(512)} %level_hbm.1, bf16[1024,1024]{1,0:T(8,128)(2,1)} %constant.4.clone.table_hbm, ...), custom_call_target="tpu_custom_call" | custom-call | tf_op jit(solution)/shard_map/pallas_call | solution.py:373
  51.5 1.0 %shard_map.78 = (f32[2,128,1024]{2,1,0:T(8,128)}, f32[2]{0:T(128)}) custom-call(f32[2,128,1024]{2,1,0:T(8,128)S(1)} %get-tuple-element.4.field, f32[2,8,128]{2,1,0:T(8,128)S(1)} %get-tuple-element.5.total), custom_call_target="tpu_custom_call" | custom-call | tf_op jit(solution)/shard_map/pallas_call | solution.py:420

commit v6 on v5

--- a/solution.py
+++ b/solution.py
@@ -194,53 +194,44 @@
 
     pl.semaphore_wait(plane_sem, rings - 1)
 
-    upper = lax.broadcasted_iota(jnp.int32, (ring // 2, 8, receivers), 1) < 4
-
-    def planes(h, offsets):
-        field = stepped[...]
-        starts = [pl.multiple_of((h * n + (z + dz) % rings * ring) * 4, 4 * ring) for dz in offsets]
-        rows = jnp.concatenate([table[pl.ds(start, 4 * ring), :] for start in starts], axis=0)
-        got = lax.dot_general(rows, field, (((1,), (1,)), ((), ())), preferred_element_type=jnp.float32)
-        for j, dz in enumerate(offsets):
-            pairs = got[j * 4 * ring : (j + 1) * 4 * ring].reshape(ring // 2, 8, shots * receivers)
-            g0, g1 = pairs[:, :, :receivers], pairs[:, :, receivers:]
-            even = jnp.where(upper, g0, pltpu.roll(g1, 4, 1))
-            odd = jnp.where(upper, pltpu.roll(g0, 4, 1), g1)
-            tiles = jnp.stack([even, odd], axis=1).reshape(ring, 8, receivers)
-            send1[h, pl.ds((z + dz) % rings * ring, ring)] = tiles.astype(jnp.bfloat16)
-
-    def send_shell(hops, src, dst, ssem, rsem):
-        for far_z in range(half + 1):
-            far_y = hops - far_z
-            if not 0 <= far_y <= half:
-                continue
-            both_z, both_y = far_z % half > 0, far_y % half > 0
-
-            def one(i, carry):
-                dz, dy = far_z, far_y
-                rest_of = i // 2
-                if both_y:
-                    dy = far_y + lax.rem(rest_of, 2) * (rings - 2 * far_y)
-                    rest_of = rest_of // 2
-                if both_z:
-                    dz = far_z + rest_of * (rings - 2 * far_z)
-                peer = lax.rem(z + dz, rings) * ring + lax.rem(place // 2 + dy, rings) * 2 + lax.rem(place + i, 2)
-                pltpu.make_async_remote_copy(
-                    src(peer), dst(me), ssem, rsem, device_id={"shot": peer}, device_id_type=MESH
-                ).start()
-                return carry
-
-            if hops == 0:
-                pltpu.make_async_copy(src(me), dst(me), rsem).start()
-            lax.fori_loop(1 if hops == 0 else 0, 2 * (1 + both_z) * (1 + both_y), one, 0)
-
     half = rings // 2
-    for h in range(halves):
-        for hops in range(2 * half, -1, -1):
-            near = hops - half
-            if near >= 0:
-                planes(h, sorted({near, (rings - near) % rings}))
-            send_shell(hops, lambda d: send1.at[h, d], lambda d: recv1.at[h, d], send1_sem.at[h], recv1_sem.at[h])
+    place_y, core = place // 2, place % 2
+    at_z = [lax.rem(z + dz, rings) * ring for dz in range(rings)]
+    at_y = [lax.rem(place_y + dy, rings) * 2 for dy in range(rings)]
+    at_core = [core, 1 - core]
+    peers = [
+        at_z[dz] + at_y[dy] + at_core[dc]
+        for hops in range(2 * half, -1, -1)
+        for far_z in range(half + 1)
+        for far_y in range(half + 1)
+        if far_z + far_y == hops
+        for dz in sorted({far_z, (rings - far_z) % rings})
+        for dy in sorted({far_y, (rings - far_y) % rings})
+        for dc in range(2)
+        if dz or dy or dc
+    ]
+
+    def exchange(src, dst, ssem, rsem):
+        for peer in peers:
+            pltpu.make_async_remote_copy(
+                src.at[peer], dst.at[me], ssem, rsem, device_id={"shot": peer}, device_id_type=MESH
+            ).start()
+        pltpu.make_async_copy(src.at[me], dst.at[me], rsem).start()
+
+    upper = lax.broadcasted_iota(jnp.int32, (n // 2, 8, receivers), 1) < 4
+
+    def to_frequencies(h, carry):
+        rows = table[pl.ds(pl.multiple_of(h * 4 * n, 4 * n), 4 * n), :]
+        got = lax.dot_general(rows, stepped[...], (((1,), (1,)), ((), ())), preferred_element_type=jnp.float32)
+        pairs = got.reshape(n // 2, 8, shots * receivers)
+        g0, g1 = pairs[:, :, :receivers], pairs[:, :, receivers:]
+        even = jnp.where(upper, g0, pltpu.roll(g1, 4, 1))
+        odd = jnp.where(upper, pltpu.roll(g0, 4, 1), g1)
+        send1[h] = jnp.stack([even, odd], axis=1).reshape(n, 8, receivers).astype(jnp.bfloat16)
+        exchange(send1.at[h], recv1.at[h], send1_sem.at[h], recv1_sem.at[h])
+        return carry
+
+    lax.fori_loop(0, halves, to_frequencies, 0)
 
     for halo in raw_halos:
         halo.wait_recv()
@@ -277,7 +268,8 @@
     wave = cn[...]
     k = n * shots
 
-    def shrink(h):
+    def to_shots(h, carry):
+        pltpu.make_async_copy(recv1.at[h], recv1.at[h], recv1_sem.at[h]).wait()
         w1, w2 = wide1.at[h], wide2.at[h]
         w1[...] = recv1[h].astype(jnp.float32).reshape(8 * n, receivers)
         for b in range(bands // halves):
@@ -302,12 +294,10 @@
                 w2[pl.ds(s * 4 + b * 2, n, stride=8), :] = real[s * n : (s + 1) * n]
                 w2[pl.ds(s * 4 + b * 2 + 1, n, stride=8), :] = imag[s * n : (s + 1) * n]
         send2[h] = w2[...].reshape(n, 8, receivers).astype(jnp.bfloat16)
-
-    for h in range(halves):
-        pltpu.make_async_copy(recv1.at[h], recv1.at[h], recv1_sem.at[h]).wait()
-        shrink(h)
-        for hops in range(2 * half, -1, -1):
-            send_shell(hops, lambda d: send2.at[h, d], lambda d: recv2.at[h, d], send2_sem.at[h], recv2_sem.at[h])
+        exchange(send2.at[h], recv2.at[h], send2_sem.at[h], recv2_sem.at[h])
+        return carry
+
+    lax.fori_loop(0, halves, to_shots, 0)
 
     pltpu.make_async_copy(energies, energies, energy_recv).wait()
     total[...] = sum(energies[i] for i in range(patches))
@@ -326,14 +316,13 @@
     for h in range(halves):
         pltpu.make_async_copy(send1.at[h, others], send1.at[h, others], send1_sem.at[h]).wait()
 
-    first_rows = lax.broadcasted_iota(jnp.int32, (n // 2, 8, receivers), 1) < 4
     for h in range(halves):
         pltpu.make_async_copy(recv2.at[h], recv2.at[h], recv2_sem.at[h]).wait()
         pairs = recv2[h].astype(jnp.float32).reshape(n // 2, 2, 8, receivers)
         even, odd = pairs[:, 0], pairs[:, 1]
         fields = [
-            jnp.where(first_rows, even, pltpu.roll(odd, 4, 1)),
-            jnp.where(first_rows, pltpu.roll(even, 4, 1), odd),
+            jnp.where(upper, even, pltpu.roll(odd, 4, 1)),
+            jnp.where(upper, pltpu.roll(even, 4, 1), odd),
         ]
         rows = table[h * 4 * n : (h + 1) * 4 * n, :]
         for s in range(shots):

time: 52.6 us -> 50.3 us (0.956)
  Pallas kernels: 51.9 us -> 49.6 us
    pallas_call x1, Pallas kernels: 50.8 us -> 48.6 us  [local(): pl.pallas_call(functools.partial(kernel, dims), out_shape=(jax.ShapeDtype...]
where the time goes in v6:
time: 50.3 us; the launch traced here: 50.2 us
  Pallas kernels  49.6 us (99%)
  between operations  0.64 us (1%)
    pallas_call x1, Pallas kernels, local(): pl.pallas_call(functools.partial(kernel, dims), out_shape=(jax.ShapeDtype...  48.6 us

profile of v6, /device:TPU:1, one launch (start us, length us, event | category | flops | bytes accessed | tf_op | source)
XLA Modules:
  0.0 50.2 jit_solution(17606128371760190331)
XLA Ops:
  0.6 48.6 %shard_map.77 = (f32[2,128,1024]{2,1,0:T(8,128)S(1)}, f32[2,8,128]{2,1,0:T(8,128)S(1)}) custom-call(bf16[2,128,1024]{2,1,0:T(8,128)(2,1)} %est_hbm.1, bf16[2,128,1024]{2,1,0:T(8,128)(2,1)} %obs_hbm.1, s32[256]{0:T(256)} %delay_hbm.1, f32[512]{0:T(512)} %level_hbm.1, bf16[1024,1024]{1,0:T(8,128)(2,1)} %constant.4.clone.table_hbm, ...), custom_call_target="tpu_custom_call" | custom-call | tf_op jit(solution)/shard_map/pallas_call | solution.py:362
  49.2 1.0 %shard_map.78 = (f32[2,128,1024]{2,1,0:T(8,128)}, f32[2]{0:T(128)}) custom-call(f32[2,128,1024]{2,1,0:T(8,128)S(1)} %get-tuple-element.4.field, f32[2,8,128]{2,1,0:T(8,128)S(1)} %get-tuple-element.5.total), custom_call_target="tpu_custom_call" | custom-call | tf_op jit(solution)/shard_map/pallas_call | solution.py:409

commit v7 on v6

--- a/solution.py
+++ b/solution.py
@@ -17,11 +17,10 @@
 MESH = pl.DeviceIdType.MESH
 
 
-def time_table(frequencies, samples, n, halves):
+def time_table(frequencies, samples):
     phase = np.arange(frequencies)[:, None] * np.arange(samples)[None, :] % samples
     angle = 2.0 * math.pi * phase / samples
     table = np.stack([np.cos(angle), -np.sin(angle)], axis=1) / math.sqrt(samples)
-    table = table.reshape(n, halves, -1, samples).swapaxes(0, 1)
     return table.reshape(2 * frequencies, samples).astype(np.float32).astype(ml_dtypes.bfloat16)
 
 
@@ -54,8 +53,9 @@
     patches, n, rings, ring = dims
     shots, receivers, length = est.shape
     rest = length - LONGEST
-    halves = wide1.shape[0]
-    bands = 2 * halves
+    halves = stepped.shape[0]
+    part = receivers // halves
+    bands = table.shape[0] // 2 // n
     me, x = lax.axis_index("shot"), lax.axis_index("patch")
     z, place = me // ring, me % ring
     right, left = (me + 1) % n, (me + n - 1) % n
@@ -183,14 +183,11 @@
         from_right = jnp.where(has_right, halo_in[1, rows, :].astype(jnp.float32), 0.0)
         h0 = jnp.concatenate([from_left[:, :LONGEST], -from_right[:, LONGEST:]], axis=1)
         h1 = jnp.concatenate([-from_left[:, LONGEST:], from_right[:, :LONGEST]], axis=1)
-        stepped[rows, :] = (base[0, rows, :] + 0.5 * h0).astype(jnp.bfloat16)
-        stepped[pl.ds(receivers + i * ROWS, ROWS), :] = (base[1, rows, :] + 0.5 * h1).astype(jnp.bfloat16)
-        return carry
-
-    for block in range(BLOCKS):
-        for halo in halo_copies(block):
-            halo.wait_recv()
-        lax.fori_loop(block * steps, (block + 1) * steps, after_halo, 0)
+        h, r = i // (part // ROWS), lax.rem(i, part // ROWS) * ROWS
+        stepped[h, pl.ds(r, ROWS), :] = (base[0, rows, :] + 0.5 * h0).astype(jnp.bfloat16)
+        stepped[h, pl.ds(part + r, ROWS), :] = (base[1, rows, :] + 0.5 * h1).astype(jnp.bfloat16)
+        return carry
+
 
     pl.semaphore_wait(plane_sem, rings - 1)
 
@@ -218,16 +215,14 @@
             ).start()
         pltpu.make_async_copy(src.at[me], dst.at[me], rsem).start()
 
-    upper = lax.broadcasted_iota(jnp.int32, (n // 2, 8, receivers), 1) < 4
-
     def to_frequencies(h, carry):
-        rows = table[pl.ds(pl.multiple_of(h * 4 * n, 4 * n), 4 * n), :]
-        got = lax.dot_general(rows, stepped[...], (((1,), (1,)), ((), ())), preferred_element_type=jnp.float32)
-        pairs = got.reshape(n // 2, 8, shots * receivers)
-        g0, g1 = pairs[:, :, :receivers], pairs[:, :, receivers:]
-        even = jnp.where(upper, g0, pltpu.roll(g1, 4, 1))
-        odd = jnp.where(upper, pltpu.roll(g0, 4, 1), g1)
-        send1[h] = jnp.stack([even, odd], axis=1).reshape(n, 8, receivers).astype(jnp.bfloat16)
+        for j in range(BLOCKS // halves):
+            block = h * (BLOCKS // halves) + j
+            for halo in halo_copies(block):
+                halo.wait_recv()
+            lax.fori_loop(block * steps, (block + 1) * steps, after_halo, 0)
+        got = lax.dot_general(table[...], stepped[h], (((1,), (1,)), ((), ())), preferred_element_type=jnp.float32)
+        send1[h] = got.reshape(n, 8, receivers).astype(jnp.bfloat16)
         exchange(send1.at[h], recv1.at[h], send1_sem.at[h], recv1_sem.at[h])
         return carry
 
@@ -268,31 +263,44 @@
     wave = cn[...]
     k = n * shots
 
+    low = lax.broadcasted_iota(jnp.int32, (n, receivers), 1) < part
+    sign = jnp.where(lax.broadcasted_iota(jnp.int32, (k, receivers), 1) < part, 1.0, -1.0)
+
+    def swapped(v):
+        return pltpu.roll(v, part, 1)
+
+    def exchanged(v0, v1):
+        return jnp.where(low, v0, swapped(v1)), jnp.where(low, swapped(v0), v1)
+
     def to_shots(h, carry):
         pltpu.make_async_copy(recv1.at[h], recv1.at[h], recv1_sem.at[h]).wait()
         w1, w2 = wide1.at[h], wide2.at[h]
         w1[...] = recv1[h].astype(jnp.float32).reshape(8 * n, receivers)
-        for b in range(bands // halves):
+        for pair in range(0, bands, 2):
             columns = []
-            for q in range(2):
-                parts = [w1[pl.ds(s * 4 + b * 2 + q, n, stride=8), :] for s in range(shots)]
-                columns.append(jnp.concatenate(parts, axis=0))
+            for b in (pair, pair + 1):
+                cut = [w1[pl.ds(b * 2 + q, n, stride=8), :] for q in range(2)]
+                columns.append(jnp.concatenate(exchanged(*cut), axis=0))
             field = jnp.concatenate(columns, axis=1).astype(jnp.bfloat16)
             got = jnp.dot(wave, field, preferred_element_type=jnp.float32)
-            real = got[:k, :receivers] + got[k:, receivers:]
-            imag = got[:k, receivers:] - got[k:, :receivers]
-            f = me * bands + h * (bands // halves) + b
-            limit = level[f]
-            weight = jnp.where(f == 0, 1.0, 2.0)
-            magnitude = jnp.sqrt(real * real + imag * imag)
-            factor = jnp.maximum(magnitude - limit, 0.0) / jnp.maximum(magnitude, limit) * weight
-            shrunk = jnp.concatenate([real * factor, imag * factor], axis=1).astype(jnp.bfloat16)
+            columns = []
+            for i, b in enumerate((pair, pair + 1)):
+                lanes = slice(i * receivers, (i + 1) * receivers)
+                v = got[:k, lanes] + sign * swapped(got[k:, lanes])
+                f = me * bands + b
+                limit = level[f]
+                weight = jnp.where(f == 0, 1.0, 2.0)
+                squares = v * v
+                magnitude = jnp.sqrt(squares + swapped(squares))
+                factor = jnp.maximum(magnitude - limit, 0.0) / jnp.maximum(magnitude, limit) * weight
+                columns.append(v * factor)
+            shrunk = jnp.concatenate(columns, axis=1).astype(jnp.bfloat16)
             got = jnp.dot(wave, shrunk, preferred_element_type=jnp.float32)
-            real = got[:k, :receivers] - got[k:, receivers:]
-            imag = got[:k, receivers:] + got[k:, :receivers]
-            for s in range(shots):
-                w2[pl.ds(s * 4 + b * 2, n, stride=8), :] = real[s * n : (s + 1) * n]
-                w2[pl.ds(s * 4 + b * 2 + 1, n, stride=8), :] = imag[s * n : (s + 1) * n]
+            for i, b in enumerate((pair, pair + 1)):
+                lanes = slice(i * receivers, (i + 1) * receivers)
+                v = got[:k, lanes] - sign * swapped(got[k:, lanes])
+                for p, cut in enumerate(exchanged(v[:n], v[n:])):
+                    w2[pl.ds(b * 2 + p, n, stride=8), :] = cut
         send2[h] = w2[...].reshape(n, 8, receivers).astype(jnp.bfloat16)
         exchange(send2.at[h], recv2.at[h], send2_sem.at[h], recv2_sem.at[h])
         return carry
@@ -316,19 +324,15 @@
     for h in range(halves):
         pltpu.make_async_copy(send1.at[h, others], send1.at[h, others], send1_sem.at[h]).wait()
 
-    for h in range(halves):
+    def to_samples(h, carry):
         pltpu.make_async_copy(recv2.at[h], recv2.at[h], recv2_sem.at[h]).wait()
-        pairs = recv2[h].astype(jnp.float32).reshape(n // 2, 2, 8, receivers)
-        even, odd = pairs[:, 0], pairs[:, 1]
-        fields = [
-            jnp.where(upper, even, pltpu.roll(odd, 4, 1)),
-            jnp.where(upper, pltpu.roll(even, 4, 1), odd),
-        ]
-        rows = table[h * 4 * n : (h + 1) * 4 * n, :]
+        field = recv2[h].astype(jnp.float32).reshape(8 * n, receivers).astype(jnp.bfloat16)
+        got = lax.dot_general(field, table[...], (((0,), (0,)), ((), ())), preferred_element_type=jnp.float32)
         for s in range(shots):
-            field = fields[s].reshape(4 * n, receivers).astype(jnp.bfloat16)
-            got = lax.dot_general(field, rows, (((0,), (0,)), ((), ())), preferred_element_type=jnp.float32)
-            out[s] = got if h == 0 else out[s] + got
+            out[s, pl.ds(pl.multiple_of(h * part, part), part), :] = got[s * part : (s + 1) * part]
+        return carry
+
+    lax.fori_loop(0, halves, to_samples, 0)
 
     for h in range(halves):
         pltpu.make_async_copy(send2.at[h, others], send2.at[h, others], send2_sem.at[h]).wait()
@@ -352,9 +356,8 @@
     n = dims[1]
     frequencies = thresholds.shape[0]
     bf16, f32 = jnp.bfloat16, jnp.float32
-    bands = frequencies // n
-    halves = bands // 2
-    table = jnp.asarray(time_table(frequencies, length, n, halves))
+    halves = 2
+    table = jnp.asarray(time_table(frequencies, length))
     cn = jnp.asarray(shot_table(n * shots, shots))
     sem = pltpu.SemaphoreType.DMA
     vmem = pl.BlockSpec(memory_space=pltpu.VMEM)
@@ -379,7 +382,7 @@
             pltpu.VMEM((2, receivers, LONGEST), bf16),
             pltpu.VMEM(estimate.shape, f32),
             pltpu.VMEM(estimate.shape, f32),
-            pltpu.VMEM((shots * receivers, length), bf16),
+            pltpu.VMEM((halves, shots * receivers // halves, length), bf16),
             pltpu.VMEM((shots, 8, 128), f32),
             pltpu.VMEM((dims[0], shots, 8, 128), f32),
             pltpu.VMEM((halves, n, 8, receivers), bf16),

time: 50.3 us -> 51.7 us (1.028)
  Pallas kernels: 49.6 us -> 50.9 us
    pallas_call x1, Pallas kernels: 48.6 us -> 49.9 us  [local(): pl.pallas_call(functools.partial(kernel, dims), out_shape=(jax.ShapeDtype...]
where the time goes in v7:
time: 51.7 us; the launch traced here: 51.6 us
  Pallas kernels  50.9 us (98%)
  between operations  0.64 us (1%)
    pallas_call x1, Pallas kernels, local(): pl.pallas_call(functools.partial(kernel, dims), out_shape=(jax.ShapeDtype...  49.9 us

profile of v7, /device:TPU:1, one launch (start us, length us, event | category | flops | bytes accessed | tf_op | source)
XLA Modules:
  0.0 51.6 jit_solution(9076802678349476531)
XLA Ops:
  0.6 49.9 %shard_map.77 = (f32[2,128,1024]{2,1,0:T(8,128)S(1)}, f32[2,8,128]{2,1,0:T(8,128)S(1)}) custom-call(bf16[2,128,1024]{2,1,0:T(8,128)(2,1)} %est_hbm.1, bf16[2,128,1024]{2,1,0:T(8,128)(2,1)} %obs_hbm.1, s32[256]{0:T(256)} %delay_hbm.1, f32[512]{0:T(512)} %level_hbm.1, bf16[1024,1024]{1,0:T(8,128)(2,1)} %constant.4.clone.table_hbm, ...), custom_call_target="tpu_custom_call" | custom-call | tf_op jit(solution)/shard_map/pallas_call | solution.py:365
  50.6 1.0 %shard_map.78 = (f32[2,128,1024]{2,1,0:T(8,128)}, f32[2]{0:T(128)}) custom-call(f32[2,128,1024]{2,1,0:T(8,128)S(1)} %get-tuple-element.4.field, f32[2,8,128]{2,1,0:T(8,128)S(1)} %get-tuple-element.5.total), custom_call_target="tpu_custom_call" | custom-call | tf_op jit(solution)/shard_map/pallas_call | solution.py:412

commit v8 on v7

--- a/solution.py
+++ b/solution.py
@@ -47,7 +47,7 @@
     est, obs, delay, level, table, cn,
     halo_out, halo_in, est_in, partial, base, stepped, energy, energies,
     send1, recv1, wide1, wide2, send2, recv2,
-    load_sem, record_sem, halo_send, halo_recv, est_send, est_recv, plane_sem,
+    load_sem, record_sem, halo_send, halo_recv, est_send, est_recv, wave_sem,
     send1_sem, recv1_sem, send2_sem, recv2_sem, energy_send, energy_recv,
 ):
     patches, n, rings, ring = dims
@@ -86,10 +86,6 @@
         pl.semaphore_signal(barrier, 1, device_id={"shot": z * ring + (place + i) % ring}, device_id_type=MESH)
         return carry
 
-    def greet_planes(i, carry):
-        pl.semaphore_signal(barrier, 1, device_id={"shot": (z + i) % rings * ring + place}, device_id_type=MESH)
-        return carry
-
     def greet_patches(i, carry):
         pl.semaphore_signal(barrier, 1, device_id={"patch": (x + i) % patches}, device_id_type=MESH)
         return carry
@@ -97,7 +93,17 @@
     pl.semaphore_signal(barrier, 1, device_id={"shot": right}, device_id_type=MESH)
     pl.semaphore_signal(barrier, 1, device_id={"shot": left}, device_id_type=MESH)
     lax.fori_loop(1, ring, greet_ring, 0)
-    lax.fori_loop(1, rings, greet_planes, 0)
+
+    def tell(sem, reach):
+        for there, inside in [(z + reach, z + reach < rings), (z - reach, z >= reach)]:
+
+            @pl.when(inside)
+            def _():
+                pl.semaphore_signal(sem, 1, device_id={"shot": there * ring + place}, device_id_type=MESH)
+
+        return jnp.where(z + reach < rings, 1, 0) + jnp.where(z >= reach, 1, 0)
+
+    beside = tell(barrier, 1)
     lax.fori_loop(1, patches, greet_patches, 0)
 
     loads[0].wait()
@@ -141,7 +147,8 @@
             load.wait()
         lax.fori_loop(block * steps, (block + 1) * steps, before_halo, 0)
         if block == 0:
-            pl.semaphore_wait(barrier, ring - 1 + rings - 1 + patches - 1 + 2)
+            pl.semaphore_wait(barrier, ring - 1 + patches - 1 + 2 + beside)
+            tell(wave_sem.at[0], 1)
         for halo in halo_copies(block):
             halo.start()
 
@@ -154,12 +161,6 @@
     ]
     for halo in raw_halos:
         halo.start()
-
-    def plane_ready(i, carry):
-        pl.semaphore_signal(plane_sem, 1, device_id={"shot": (z + i) % rings * ring + place}, device_id_type=MESH)
-        return carry
-
-    lax.fori_loop(1, rings, plane_ready, 0)
 
     def own_part(i, carry):
         rows = pl.ds(i * ROWS, ROWS)
@@ -189,7 +190,10 @@
         return carry
 
 
-    pl.semaphore_wait(plane_sem, rings - 1)
+    pl.semaphore_wait(wave_sem.at[0], beside)
+    two_away = tell(wave_sem.at[1], 2)
+    pl.semaphore_wait(wave_sem.at[1], two_away)
+    four_away = tell(wave_sem.at[2], 4)
 
     half = rings // 2
     place_y, core = place // 2, place % 2
@@ -215,7 +219,7 @@
             ).start()
         pltpu.make_async_copy(src.at[me], dst.at[me], rsem).start()
 
-    def to_frequencies(h, carry):
+    def to_frequencies(h):
         for j in range(BLOCKS // halves):
             block = h * (BLOCKS // halves) + j
             for halo in halo_copies(block):
@@ -223,10 +227,53 @@
             lax.fori_loop(block * steps, (block + 1) * steps, after_halo, 0)
         got = lax.dot_general(table[...], stepped[h], (((1,), (1,)), ((), ())), preferred_element_type=jnp.float32)
         send1[h] = got.reshape(n, 8, receivers).astype(jnp.bfloat16)
-        exchange(send1.at[h], recv1.at[h], send1_sem.at[h], recv1_sem.at[h])
-        return carry
-
-    lax.fori_loop(0, halves, to_frequencies, 0)
+        pltpu.make_async_copy(send1.at[h, me], recv1.at[h, me], recv1_sem.at[h]).start()
+
+    def send_planes(h, start, stop):
+        def one(zz, carry):
+            def send(dy, dc):
+                peer = zz * ring + at_y[dy] + at_core[dc]
+                pltpu.make_async_remote_copy(
+                    send1.at[h, peer], recv1.at[h, me], send1_sem.at[h], recv1_sem.at[h],
+                    device_id={"shot": peer}, device_id_type=MESH,
+                ).start()
+
+            for dy in sorted(range(rings), key=lambda d: -min(d, rings - d)):
+                for dc in range(2):
+                    if dy or dc:
+                        send(dy, dc)
+
+            @pl.when(zz != z)
+            def _():
+                send(0, 0)
+
+            return carry
+
+        lax.fori_loop(start, stop, one, 0)
+
+    def send_near(h):
+        send_planes(h, jnp.maximum(z - 3, 0), jnp.minimum(z + 4, rings))
+
+    def send_far(h):
+        send_planes(h, jnp.where(z < half, z + 4, 0), jnp.where(z < half, rings, z - 3))
+
+    to_frequencies(0)
+    send_near(0)
+
+    @pl.when(z >= half)
+    def _():
+        pl.semaphore_wait(wave_sem.at[2], four_away)
+        send_far(0)
+
+    to_frequencies(1)
+    send_near(1)
+
+    @pl.when(z < half)
+    def _():
+        pl.semaphore_wait(wave_sem.at[2], four_away)
+        send_far(0)
+
+    send_far(1)
 
     for halo in raw_halos:
         halo.wait_recv()
@@ -264,7 +311,7 @@
     k = n * shots
 
     low = lax.broadcasted_iota(jnp.int32, (n, receivers), 1) < part
-    sign = jnp.where(lax.broadcasted_iota(jnp.int32, (k, receivers), 1) < part, 1.0, -1.0)
+    low_k = lax.broadcasted_iota(jnp.int32, (k, receivers), 1) < part
 
     def swapped(v):
         return pltpu.roll(v, part, 1)
@@ -278,28 +325,24 @@
         w1[...] = recv1[h].astype(jnp.float32).reshape(8 * n, receivers)
         for pair in range(0, bands, 2):
             columns = []
-            for b in (pair, pair + 1):
-                cut = [w1[pl.ds(b * 2 + q, n, stride=8), :] for q in range(2)]
+            for q in range(2):
+                cut = [w1[pl.ds(b * 2 + q, n, stride=8), :] for b in (pair, pair + 1)]
                 columns.append(jnp.concatenate(exchanged(*cut), axis=0))
             field = jnp.concatenate(columns, axis=1).astype(jnp.bfloat16)
             got = jnp.dot(wave, field, preferred_element_type=jnp.float32)
-            columns = []
-            for i, b in enumerate((pair, pair + 1)):
-                lanes = slice(i * receivers, (i + 1) * receivers)
-                v = got[:k, lanes] + sign * swapped(got[k:, lanes])
-                f = me * bands + b
-                limit = level[f]
-                weight = jnp.where(f == 0, 1.0, 2.0)
-                squares = v * v
-                magnitude = jnp.sqrt(squares + swapped(squares))
-                factor = jnp.maximum(magnitude - limit, 0.0) / jnp.maximum(magnitude, limit) * weight
-                columns.append(v * factor)
-            shrunk = jnp.concatenate(columns, axis=1).astype(jnp.bfloat16)
+            real = got[:k, :receivers] + got[k:, receivers:]
+            imag = got[:k, receivers:] - got[k:, :receivers]
+            f = me * bands + pair
+            limit = jnp.where(low_k, level[f], level[f + 1])
+            weight = jnp.where(low_k, jnp.where(f == 0, 1.0, 2.0), 2.0)
+            magnitude = jnp.sqrt(real * real + imag * imag)
+            factor = jnp.maximum(magnitude - limit, 0.0) / jnp.maximum(magnitude, limit) * weight
+            shrunk = jnp.concatenate([real * factor, imag * factor], axis=1).astype(jnp.bfloat16)
             got = jnp.dot(wave, shrunk, preferred_element_type=jnp.float32)
-            for i, b in enumerate((pair, pair + 1)):
-                lanes = slice(i * receivers, (i + 1) * receivers)
-                v = got[:k, lanes] - sign * swapped(got[k:, lanes])
-                for p, cut in enumerate(exchanged(v[:n], v[n:])):
+            real = got[:k, :receivers] - got[k:, receivers:]
+            imag = got[:k, receivers:] + got[k:, :receivers]
+            for p, v in enumerate([real, imag]):
+                for b, cut in zip((pair, pair + 1), exchanged(v[:n], v[n:])):
                     w2[pl.ds(b * 2 + p, n, stride=8), :] = cut
         send2[h] = w2[...].reshape(n, 8, receivers).astype(jnp.bfloat16)
         exchange(send2.at[h], recv2.at[h], send2_sem.at[h], recv2_sem.at[h])
@@ -397,7 +440,7 @@
             sem((2, BLOCKS)),
             sem((2,)),
             sem((2,)),
-            pltpu.SemaphoreType.REGULAR,
+            pltpu.SemaphoreType.REGULAR((3,)),
             sem((halves,)),
             sem((halves,)),
             sem((halves,)),

time: 51.7 us -> 55.4 us (1.072)
  Pallas kernels: 50.9 us -> 54.6 us
    pallas_call x1, Pallas kernels: 49.9 us -> 53.6 us  [local(): pl.pallas_call(functools.partial(kernel, dims), out_shape=(jax.ShapeDtype...]
where the time goes in v8:
time: 55.4 us; the launch traced here: 55.2 us
  Pallas kernels  54.6 us (99%)
  between operations  0.64 us (1%)
    pallas_call x1, Pallas kernels, local(): pl.pallas_call(functools.partial(kernel, dims), out_shape=(jax.ShapeDtype...  53.6 us

profile of v8, /device:TPU:1, one launch (start us, length us, event | category | flops | bytes accessed | tf_op | source)
XLA Modules:
  0.0 55.2 jit_solution(15627891199967572651)
XLA Ops:
  0.6 53.6 %shard_map.77 = (f32[2,128,1024]{2,1,0:T(8,128)S(1)}, f32[2,8,128]{2,1,0:T(8,128)S(1)}) custom-call(bf16[2,128,1024]{2,1,0:T(8,128)(2,1)} %est_hbm.1, bf16[2,128,1024]{2,1,0:T(8,128)(2,1)} %obs_hbm.1, s32[256]{0:T(256)} %delay_hbm.1, f32[512]{0:T(512)} %level_hbm.1, bf16[1024,1024]{1,0:T(8,128)(2,1)} %constant.4.clone.table_hbm, ...), custom_call_target="tpu_custom_call" | custom-call | tf_op jit(solution)/shard_map/pallas_call | solution.py:408
  54.2 1.0 %shard_map.78 = (f32[2,128,1024]{2,1,0:T(8,128)}, f32[2]{0:T(128)}) custom-call(f32[2,128,1024]{2,1,0:T(8,128)S(1)} %get-tuple-element.4.field, f32[2,8,128]{2,1,0:T(8,128)S(1)} %get-tuple-element.5.total), custom_call_target="tpu_custom_call" | custom-call | tf_op jit(solution)/shard_map/pallas_call | solution.py:455

commit v9 on v7

--- a/solution.py
+++ b/solution.py
@@ -152,9 +152,6 @@
         )
         for side, peer in enumerate([right, left])
     ]
-    for halo in raw_halos:
-        halo.start()
-
     def plane_ready(i, carry):
         pl.semaphore_signal(plane_sem, 1, device_id={"shot": (z + i) % rings * ring + place}, device_id_type=MESH)
         return carry
@@ -224,47 +221,54 @@
         got = lax.dot_general(table[...], stepped[h], (((1,), (1,)), ((), ())), preferred_element_type=jnp.float32)
         send1[h] = got.reshape(n, 8, receivers).astype(jnp.bfloat16)
         exchange(send1.at[h], recv1.at[h], send1_sem.at[h], recv1_sem.at[h])
+
+        @pl.when(h == 0)
+        def _():
+            for halo in raw_halos:
+                halo.start()
+
         return carry
 
     lax.fori_loop(0, halves, to_frequencies, 0)
 
-    for halo in raw_halos:
-        halo.wait_recv()
-
-    def misfit_part(i, carry):
-        rows = pl.ds(i * ROWS, ROWS)
-        blank = jnp.zeros((ROWS, rest), jnp.float32)
-        from_left = jnp.concatenate([blank, est_in[0, rows, :].astype(jnp.float32)], axis=1)
-        from_right = jnp.concatenate([est_in[1, rows, :].astype(jnp.float32), blank], axis=1)
-        r0 = partial[0, rows, :] - jnp.where(has_left, shift_left(from_left, lane, a_before), 0.0)
-        r1 = partial[1, rows, :] - jnp.where(has_right, shift_right(from_right, lane, a_after), 0.0)
-
-        def squares(r):
-            parts = jnp.zeros((8, 128), jnp.float32)
-            for a in range(0, ROWS, 8):
-                for b in range(0, length, 128):
-                    piece = r[a : a + 8, b : b + 128]
-                    parts = parts + piece * piece
-            return parts
-
-        return carry[0] + squares(r0), carry[1] + squares(r1)
-
-    zero = jnp.zeros((8, 128), jnp.float32)
-    e_0, e_1 = lax.fori_loop(0, receivers // ROWS, misfit_part, (zero, zero))
-    energy[0] = e_0
-    energy[1] = e_1
-    for i in range(1, patches):
-        pltpu.make_async_remote_copy(
-            energy, energies.at[x], energy_send.at[i], energy_recv,
-            device_id={"patch": (x + i) % patches}, device_id_type=MESH,
-        ).start()
-    pltpu.make_async_copy(energy, energies.at[x], energy_recv).start()
+    def own_misfit():
+        for halo in raw_halos:
+            halo.wait_recv()
+
+        def misfit_part(i, carry):
+            rows = pl.ds(i * ROWS, ROWS)
+            blank = jnp.zeros((ROWS, rest), jnp.float32)
+            from_left = jnp.concatenate([blank, est_in[0, rows, :].astype(jnp.float32)], axis=1)
+            from_right = jnp.concatenate([est_in[1, rows, :].astype(jnp.float32), blank], axis=1)
+            r0 = partial[0, rows, :] - jnp.where(has_left, shift_left(from_left, lane, a_before), 0.0)
+            r1 = partial[1, rows, :] - jnp.where(has_right, shift_right(from_right, lane, a_after), 0.0)
+
+            def squares(r):
+                parts = jnp.zeros((8, 128), jnp.float32)
+                for a in range(0, ROWS, 8):
+                    for b in range(0, length, 128):
+                        piece = r[a : a + 8, b : b + 128]
+                        parts = parts + piece * piece
+                return parts
+
+            return carry[0] + squares(r0), carry[1] + squares(r1)
+
+        zero = jnp.zeros((8, 128), jnp.float32)
+        e_0, e_1 = lax.fori_loop(0, receivers // ROWS, misfit_part, (zero, zero))
+        energy[0] = e_0
+        energy[1] = e_1
+        for i in range(1, patches):
+            pltpu.make_async_remote_copy(
+                energy, energies.at[x], energy_send.at[i], energy_recv,
+                device_id={"patch": (x + i) % patches}, device_id_type=MESH,
+            ).start()
+        pltpu.make_async_copy(energy, energies.at[x], energy_recv).start()
 
     wave = cn[...]
     k = n * shots
 
     low = lax.broadcasted_iota(jnp.int32, (n, receivers), 1) < part
-    sign = jnp.where(lax.broadcasted_iota(jnp.int32, (k, receivers), 1) < part, 1.0, -1.0)
+    low_k = lax.broadcasted_iota(jnp.int32, (k, receivers), 1) < part
 
     def swapped(v):
         return pltpu.roll(v, part, 1)
@@ -278,31 +282,28 @@
         w1[...] = recv1[h].astype(jnp.float32).reshape(8 * n, receivers)
         for pair in range(0, bands, 2):
             columns = []
-            for b in (pair, pair + 1):
-                cut = [w1[pl.ds(b * 2 + q, n, stride=8), :] for q in range(2)]
+            for q in range(2):
+                cut = [w1[pl.ds(b * 2 + q, n, stride=8), :] for b in (pair, pair + 1)]
                 columns.append(jnp.concatenate(exchanged(*cut), axis=0))
             field = jnp.concatenate(columns, axis=1).astype(jnp.bfloat16)
             got = jnp.dot(wave, field, preferred_element_type=jnp.float32)
-            columns = []
-            for i, b in enumerate((pair, pair + 1)):
-                lanes = slice(i * receivers, (i + 1) * receivers)
-                v = got[:k, lanes] + sign * swapped(got[k:, lanes])
-                f = me * bands + b
-                limit = level[f]
-                weight = jnp.where(f == 0, 1.0, 2.0)
-                squares = v * v
-                magnitude = jnp.sqrt(squares + swapped(squares))
-                factor = jnp.maximum(magnitude - limit, 0.0) / jnp.maximum(magnitude, limit) * weight
-                columns.append(v * factor)
-            shrunk = jnp.concatenate(columns, axis=1).astype(jnp.bfloat16)
+            real = got[:k, :receivers] + got[k:, receivers:]
+            imag = got[:k, receivers:] - got[k:, :receivers]
+            f = me * bands + pair
+            limit = jnp.where(low_k, level[f], level[f + 1])
+            weight = jnp.where(low_k, jnp.where(f == 0, 1.0, 2.0), 2.0)
+            magnitude = jnp.sqrt(real * real + imag * imag)
+            factor = jnp.maximum(magnitude - limit, 0.0) / jnp.maximum(magnitude, limit) * weight
+            shrunk = jnp.concatenate([real * factor, imag * factor], axis=1).astype(jnp.bfloat16)
             got = jnp.dot(wave, shrunk, preferred_element_type=jnp.float32)
-            for i, b in enumerate((pair, pair + 1)):
-                lanes = slice(i * receivers, (i + 1) * receivers)
-                v = got[:k, lanes] - sign * swapped(got[k:, lanes])
-                for p, cut in enumerate(exchanged(v[:n], v[n:])):
+            real = got[:k, :receivers] - got[k:, receivers:]
+            imag = got[:k, receivers:] + got[k:, :receivers]
+            for p, v in enumerate([real, imag]):
+                for b, cut in zip((pair, pair + 1), exchanged(v[:n], v[n:])):
                     w2[pl.ds(b * 2 + p, n, stride=8), :] = cut
         send2[h] = w2[...].reshape(n, 8, receivers).astype(jnp.bfloat16)
         exchange(send2.at[h], recv2.at[h], send2_sem.at[h], recv2_sem.at[h])
+        pl.when(h == 0)(own_misfit)
         return carry
 
     lax.fori_loop(0, halves, to_shots, 0)

time: 51.7 us -> 52.6 us (1.017)
  Pallas kernels: 50.9 us -> 51.8 us
    pallas_call x1, Pallas kernels: 49.9 us -> 50.8 us  [local(): pl.pallas_call(functools.partial(kernel, dims), out_shape=(jax.ShapeDtype...]
where the time goes in v9:
time: 52.6 us; the launch traced here: 52.4 us
  Pallas kernels  51.8 us (98%)
  between operations  0.64 us (1%)
    pallas_call x1, Pallas kernels, local(): pl.pallas_call(functools.partial(kernel, dims), out_shape=(jax.ShapeDtype...  50.8 us

profile of v9, /device:TPU:1, one launch (start us, length us, event | category | flops | bytes accessed | tf_op | source)
XLA Modules:
  0.0 52.4 jit_solution(4813255805792071409)
XLA Ops:
  0.6 50.8 %shard_map.77 = (f32[2,128,1024]{2,1,0:T(8,128)S(1)}, f32[2,8,128]{2,1,0:T(8,128)S(1)}) custom-call(bf16[2,128,1024]{2,1,0:T(8,128)(2,1)} %est_hbm.1, bf16[2,128,1024]{2,1,0:T(8,128)(2,1)} %obs_hbm.1, s32[256]{0:T(256)} %delay_hbm.1, f32[512]{0:T(512)} %level_hbm.1, bf16[1024,1024]{1,0:T(8,128)(2,1)} %constant.4.clone.table_hbm, ...), custom_call_target="tpu_custom_call" | custom-call | tf_op jit(solution)/shard_map/pallas_call | solution.py:366
  51.4 1.0 %shard_map.78 = (f32[2,128,1024]{2,1,0:T(8,128)}, f32[2]{0:T(128)}) custom-call(f32[2,128,1024]{2,1,0:T(8,128)S(1)} %get-tuple-element.4.field, f32[2,8,128]{2,1,0:T(8,128)S(1)} %get-tuple-element.5.total), custom_call_target="tpu_custom_call" | custom-call | tf_op jit(solution)/shard_map/pallas_call | solution.py:413

commit v10 on v7

--- a/solution.py
+++ b/solution.py
@@ -264,7 +264,7 @@
     k = n * shots
 
     low = lax.broadcasted_iota(jnp.int32, (n, receivers), 1) < part
-    sign = jnp.where(lax.broadcasted_iota(jnp.int32, (k, receivers), 1) < part, 1.0, -1.0)
+    low_k = lax.broadcasted_iota(jnp.int32, (k, receivers), 1) < part
 
     def swapped(v):
         return pltpu.roll(v, part, 1)
@@ -278,28 +278,24 @@
         w1[...] = recv1[h].astype(jnp.float32).reshape(8 * n, receivers)
         for pair in range(0, bands, 2):
             columns = []
-            for b in (pair, pair + 1):
-                cut = [w1[pl.ds(b * 2 + q, n, stride=8), :] for q in range(2)]
+            for q in range(2):
+                cut = [w1[pl.ds(b * 2 + q, n, stride=8), :] for b in (pair, pair + 1)]
                 columns.append(jnp.concatenate(exchanged(*cut), axis=0))
             field = jnp.concatenate(columns, axis=1).astype(jnp.bfloat16)
             got = jnp.dot(wave, field, preferred_element_type=jnp.float32)
-            columns = []
-            for i, b in enumerate((pair, pair + 1)):
-                lanes = slice(i * receivers, (i + 1) * receivers)
-                v = got[:k, lanes] + sign * swapped(got[k:, lanes])
-                f = me * bands + b
-                limit = level[f]
-                weight = jnp.where(f == 0, 1.0, 2.0)
-                squares = v * v
-                magnitude = jnp.sqrt(squares + swapped(squares))
-                factor = jnp.maximum(magnitude - limit, 0.0) / jnp.maximum(magnitude, limit) * weight
-                columns.append(v * factor)
-            shrunk = jnp.concatenate(columns, axis=1).astype(jnp.bfloat16)
+            real = got[:k, :receivers] + got[k:, receivers:]
+            imag = got[:k, receivers:] - got[k:, :receivers]
+            f = me * bands + pair
+            limit = jnp.where(low_k, level[f], level[f + 1])
+            weight = jnp.where(low_k, jnp.where(f == 0, 1.0, 2.0), 2.0)
+            magnitude = jnp.sqrt(real * real + imag * imag)
+            factor = jnp.maximum(magnitude - limit, 0.0) / jnp.maximum(magnitude, limit) * weight
+            shrunk = jnp.concatenate([real * factor, imag * factor], axis=1).astype(jnp.bfloat16)
             got = jnp.dot(wave, shrunk, preferred_element_type=jnp.float32)
-            for i, b in enumerate((pair, pair + 1)):
-                lanes = slice(i * receivers, (i + 1) * receivers)
-                v = got[:k, lanes] - sign * swapped(got[k:, lanes])
-                for p, cut in enumerate(exchanged(v[:n], v[n:])):
+            real = got[:k, :receivers] - got[k:, receivers:]
+            imag = got[:k, receivers:] + got[k:, :receivers]
+            for p, v in enumerate([real, imag]):
+                for b, cut in zip((pair, pair + 1), exchanged(v[:n], v[n:])):
                     w2[pl.ds(b * 2 + p, n, stride=8), :] = cut
         send2[h] = w2[...].reshape(n, 8, receivers).astype(jnp.bfloat16)
         exchange(send2.at[h], recv2.at[h], send2_sem.at[h], recv2_sem.at[h])

time: 51.7 us -> 51.4 us (level)
  no operation moved by 1% of the time
where the time goes in v10:
time: 51.4 us; the launch traced here: 51.3 us
  Pallas kernels  50.6 us (98%)
  between operations  0.64 us (1%)
    pallas_call x1, Pallas kernels, local(): pl.pallas_call(functools.partial(kernel, dims), out_shape=(jax.ShapeDtype...  49.6 us

profile of v10, /device:TPU:1, one launch (start us, length us, event | category | flops | bytes accessed | tf_op | source)
XLA Modules:
  0.0 51.3 jit_solution(16049353702849200683)
XLA Ops:
  0.6 49.6 %shard_map.77 = (f32[2,128,1024]{2,1,0:T(8,128)S(1)}, f32[2,8,128]{2,1,0:T(8,128)S(1)}) custom-call(bf16[2,128,1024]{2,1,0:T(8,128)(2,1)} %est_hbm.1, bf16[2,128,1024]{2,1,0:T(8,128)(2,1)} %obs_hbm.1, s32[256]{0:T(256)} %delay_hbm.1, f32[512]{0:T(512)} %level_hbm.1, bf16[1024,1024]{1,0:T(8,128)(2,1)} %constant.4.clone.table_hbm, ...), custom_call_target="tpu_custom_call" | custom-call | tf_op jit(solution)/shard_map/pallas_call | solution.py:361
  50.3 1.0 %shard_map.78 = (f32[2,128,1024]{2,1,0:T(8,128)}, f32[2]{0:T(128)}) custom-call(f32[2,128,1024]{2,1,0:T(8,128)S(1)} %get-tuple-element.4.field, f32[2,8,128]{2,1,0:T(8,128)S(1)} %get-tuple-element.5.total), custom_call_target="tpu_custom_call" | custom-call | tf_op jit(solution)/shard_map/pallas_call | solution.py:408

commit v11 on v6

--- a/solution.py
+++ b/solution.py
@@ -135,6 +135,10 @@
             for side, peer in enumerate([right, left])
         ]
 
+    def plane_ready(i, carry):
+        pl.semaphore_signal(plane_sem, 1, device_id={"shot": (z + i) % rings * ring + place}, device_id_type=MESH)
+        return carry
+
     steps = receivers // ROWS // BLOCKS
     for block in range(BLOCKS):
         for load in record_loads(block):
@@ -142,6 +146,7 @@
         lax.fori_loop(block * steps, (block + 1) * steps, before_halo, 0)
         if block == 0:
             pl.semaphore_wait(barrier, ring - 1 + rings - 1 + patches - 1 + 2)
+            lax.fori_loop(1, rings, plane_ready, 0)
         for halo in halo_copies(block):
             halo.start()
 
@@ -154,12 +159,6 @@
     ]
     for halo in raw_halos:
         halo.start()
-
-    def plane_ready(i, carry):
-        pl.semaphore_signal(plane_sem, 1, device_id={"shot": (z + i) % rings * ring + place}, device_id_type=MESH)
-        return carry
-
-    lax.fori_loop(1, rings, plane_ready, 0)
 
     def own_part(i, carry):
         rows = pl.ds(i * ROWS, ROWS)
@@ -192,7 +191,6 @@
             halo.wait_recv()
         lax.fori_loop(block * steps, (block + 1) * steps, after_halo, 0)
 
-    pl.semaphore_wait(plane_sem, rings - 1)
 
     half = rings // 2
     place_y, core = place // 2, place % 2
@@ -228,6 +226,11 @@
         even = jnp.where(upper, g0, pltpu.roll(g1, 4, 1))
         odd = jnp.where(upper, pltpu.roll(g0, 4, 1), g1)
         send1[h] = jnp.stack([even, odd], axis=1).reshape(n, 8, receivers).astype(jnp.bfloat16)
+
+        @pl.when(h == 0)
+        def _():
+            pl.semaphore_wait(plane_sem, rings - 1)
+
         exchange(send1.at[h], recv1.at[h], send1_sem.at[h], recv1_sem.at[h])
         return carry
 

time: 50.3 us -> 50.2 us (level)
  no operation moved by 1% of the time
where the time goes in v11:
time: 50.2 us; the launch traced here: 50.1 us
  Pallas kernels  49.4 us (98%)
  between operations  0.64 us (1%)
    pallas_call x1, Pallas kernels, local(): pl.pallas_call(functools.partial(kernel, dims), out_shape=(jax.ShapeDtype...  48.4 us

profile of v11, /device:TPU:1, one launch (start us, length us, event | category | flops | bytes accessed | tf_op | source)
XLA Modules:
  0.0 50.1 jit_solution(451256494651662751)
XLA Ops:
  0.6 48.4 %shard_map.77 = (f32[2,128,1024]{2,1,0:T(8,128)S(1)}, f32[2,8,128]{2,1,0:T(8,128)S(1)}) custom-call(bf16[2,128,1024]{2,1,0:T(8,128)(2,1)} %est_hbm.1, bf16[2,128,1024]{2,1,0:T(8,128)(2,1)} %obs_hbm.1, s32[256]{0:T(256)} %delay_hbm.1, f32[512]{0:T(512)} %level_hbm.1, bf16[1024,1024]{1,0:T(8,128)(2,1)} %constant.4.clone.table_hbm, ...), custom_call_target="tpu_custom_call" | custom-call | tf_op jit(solution)/shard_map/pallas_call | solution.py:365
  49.1 1.0 %shard_map.78 = (f32[2,128,1024]{2,1,0:T(8,128)}, f32[2]{0:T(128)}) custom-call(f32[2,128,1024]{2,1,0:T(8,128)S(1)} %get-tuple-element.4.field, f32[2,8,128]{2,1,0:T(8,128)S(1)} %get-tuple-element.5.total), custom_call_target="tpu_custom_call" | custom-call | tf_op jit(solution)/shard_map/pallas_call | solution.py:412

commit v12 on v11

--- a/solution.py
+++ b/solution.py
@@ -77,28 +77,25 @@
     for block in range(BLOCKS):
         for load in record_loads(block):
             load.start()
+
+    barrier = pltpu.get_barrier_semaphore()
+
+    def greet(**peer):
+        pl.semaphore_signal(barrier, 1, device_id=peer, device_id_type=MESH)
+
+    def far_first(size):
+        return sorted(range(1, size), key=lambda i: -min(i, size - i))
+
+    greet(shot=right)
+    greet(shot=left)
+    for i in far_first(ring):
+        greet(shot=z * ring + lax.rem(place + i, ring))
+    for i in far_first(rings):
+        greet(shot=lax.rem(z + i, rings) * ring + place)
+    for i in far_first(patches):
+        greet(patch=lax.rem(x + i, patches))
     for load in loads[1:]:
         load.start()
-
-    barrier = pltpu.get_barrier_semaphore()
-
-    def greet_ring(i, carry):
-        pl.semaphore_signal(barrier, 1, device_id={"shot": z * ring + (place + i) % ring}, device_id_type=MESH)
-        return carry
-
-    def greet_planes(i, carry):
-        pl.semaphore_signal(barrier, 1, device_id={"shot": (z + i) % rings * ring + place}, device_id_type=MESH)
-        return carry
-
-    def greet_patches(i, carry):
-        pl.semaphore_signal(barrier, 1, device_id={"patch": (x + i) % patches}, device_id_type=MESH)
-        return carry
-
-    pl.semaphore_signal(barrier, 1, device_id={"shot": right}, device_id_type=MESH)
-    pl.semaphore_signal(barrier, 1, device_id={"shot": left}, device_id_type=MESH)
-    lax.fori_loop(1, ring, greet_ring, 0)
-    lax.fori_loop(1, rings, greet_planes, 0)
-    lax.fori_loop(1, patches, greet_patches, 0)
 
     loads[0].wait()
     first = me * shots
@@ -135,10 +132,6 @@
             for side, peer in enumerate([right, left])
         ]
 
-    def plane_ready(i, carry):
-        pl.semaphore_signal(plane_sem, 1, device_id={"shot": (z + i) % rings * ring + place}, device_id_type=MESH)
-        return carry
-
     steps = receivers // ROWS // BLOCKS
     for block in range(BLOCKS):
         for load in record_loads(block):
@@ -146,7 +139,9 @@
         lax.fori_loop(block * steps, (block + 1) * steps, before_halo, 0)
         if block == 0:
             pl.semaphore_wait(barrier, ring - 1 + rings - 1 + patches - 1 + 2)
-            lax.fori_loop(1, rings, plane_ready, 0)
+            for i in far_first(rings):
+                peer = lax.rem(z + i, rings) * ring + place
+                pl.semaphore_signal(plane_sem, 1, device_id={"shot": peer}, device_id_type=MESH)
         for halo in halo_copies(block):
             halo.start()
 

time: 50.2 us -> 50.4 us (level)
  no operation moved by 1% of the time
where the time goes in v12:
time: 50.4 us; the launch traced here: 50.3 us
  Pallas kernels  49.6 us (98%)
  between operations  0.64 us (1%)
    pallas_call x1, Pallas kernels, local(): pl.pallas_call(functools.partial(kernel, dims), out_shape=(jax.ShapeDtype...  48.6 us

profile of v12, /device:TPU:1, one launch (start us, length us, event | category | flops | bytes accessed | tf_op | source)
XLA Modules:
  0.0 50.3 jit_solution(3178192994123371250)
XLA Ops:
  0.6 48.6 %shard_map.77 = (f32[2,128,1024]{2,1,0:T(8,128)S(1)}, f32[2,8,128]{2,1,0:T(8,128)S(1)}) custom-call(bf16[2,128,1024]{2,1,0:T(8,128)(2,1)} %est_hbm.1, bf16[2,128,1024]{2,1,0:T(8,128)(2,1)} %obs_hbm.1, s32[256]{0:T(256)} %delay_hbm.1, f32[512]{0:T(512)} %level_hbm.1, bf16[1024,1024]{1,0:T(8,128)(2,1)} %constant.4.clone.table_hbm, ...), custom_call_target="tpu_custom_call" | custom-call | tf_op jit(solution)/shard_map/pallas_call | solution.py:360
  49.3 1.0 %shard_map.78 = (f32[2,128,1024]{2,1,0:T(8,128)}, f32[2]{0:T(128)}) custom-call(f32[2,128,1024]{2,1,0:T(8,128)S(1)} %get-tuple-element.4.field, f32[2,8,128]{2,1,0:T(8,128)S(1)} %get-tuple-element.5.total), custom_call_target="tpu_custom_call" | custom-call | tf_op jit(solution)/shard_map/pallas_call | solution.py:407
